TPU v7x, 32 devices: a whole 2x2x4 slice. The times are simulated.
32 devices in a mesh: tm: 8 (over z, y), pix: 4 (over x, core).
Axes of the slice: x: 2, y: 2, z: 4, core: 2. Of those that a mesh axis runs over, the one named last changes fastest.
Arguments:
- counts: float32 [1024, 16384], P('tm', 'pix'), may hold values from 0.5 to 15
- dead_time: float32 [16384], P('pix'), may hold values from 0.002 to 0.03
- flat_field: float32 [16384], P('pix'), may hold values from 0.3 to 3
- cycle_map: int32 [16384], P('pix'), may hold values from 0 to 31, as said below
Outputs:
- two_time: float32 [32, 1024, 1024], P('pix', 'tm')
Inputs may be any that keep to these rules, and one draw needn't show every extreme that they name: `cycle_map`: every cycle holds at least one pixel.
All inputs are finite; a program needn't handle non-finite values.
Results may differ from a plain program's by a relative error of at most 0.00042.
Values may be sent and summed in bfloat16 or wider, within the bound.
A program may use at most 64 MiB of HBM per device.

v0:
```python
import functools
import math

import jax
import jax.numpy as jnp
from jax import lax
from jax.experimental import pallas as pl
from jax.experimental.pallas import tpu as pltpu
from jax.sharding import PartitionSpec as P

CYCLES = 32


def inner_extent(count):
    return max(d for d in range(1, count + 1) if count % d == 0 and d * d <= count)


class LogCode:
    def __init__(self, low, high, zero):
        self.low, self.zero = low, zero
        low, high = math.log2(low), math.log2(high)
        self.centre, self.steps = (high + low) / 2, 65400 / (high - low)

    def encode(self, value):
        level = (jnp.log2(jnp.maximum(value, self.low)) - self.centre) * self.steps
        return jnp.round(level).astype(jnp.int16)

    def decode(self, code):
        level = code.astype(jnp.float32)
        value = jnp.exp2(level * (1.0 / self.steps) + self.centre)
        return jnp.where(level > -32700 + 32, value, 0.0) if self.zero else value


def per_device(counts, dead_time, flat_field, cycle_map):
    intensity = (counts / (1.0 - dead_time[None, :] * counts) * flat_field[None, :]).astype(
        jnp.bfloat16
    )
    frames, pixels = intensity.shape
    tm, pix = lax.axis_size("tm"), lax.axis_size("pix")
    inner = inner_extent(tm)
    outer = tm // inner
    cores = 2 if pix % 2 == 0 else 1
    across = pix // cores
    owned = CYCLES // pix
    at_tm, at_pix = lax.axis_index("tm"), lax.axis_index("pix")
    z, y = at_tm // inner, at_tm % inner
    x, core = at_pix // cores, at_pix % cores

    def shift_z(value, k=1):
        return lax.ppermute(
            value, "tm", [(i, (i // inner + k) % outer * inner + i % inner) for i in range(tm)]
        )

    def shift_y(value, k):
        return lax.ppermute(
            value, "tm", [(i, i // inner * inner + (i % inner + k) % inner) for i in range(tm)]
        )

    def shift_x(value, k):
        return lax.ppermute(
            value, "pix", [(i, (i // cores + k) % across * cores + i % cores) for i in range(pix)]
        )

    def swap_core(value):
        return lax.ppermute(
            value, "pix", [(i, i // cores * cores + (i % cores + 1) % cores) for i in range(pix)]
        )

    half = outer // 2
    remote = {0: intensity}
    for s in range(1, half + 1):
        remote[s] = shift_z(remote[s - 1])
    beside = [intensity]
    for k in range(1, inner):
        beside.append(shift_y(intensity, k))

    def onehot_of(owner_core, ks):
        ids = jnp.concatenate(
            [
                ((x + k) % across * cores + owner_core) * owned
                + jnp.arange(owned, dtype=jnp.int32)
                for k in ks
            ]
        )
        return (cycle_map[None, :] == ids[:, None]).astype(jnp.bfloat16)

    other = (core + 1) % cores
    away_ks, own_ks = range(1, across), range(1)
    rows = frames + 8

    def gram(onehot, left, right, sums):
        masked = (onehot[:, None, :] * left[None, :, :]).reshape(-1, pixels)
        value = lax.dot_general(
            masked, right, (((1,), (1,)), ((), ())), preferred_element_type=jnp.float32
        ).reshape(onehot.shape[0], rows, right.shape[0])
        if sums is not None:
            own = lax.dot_general(
                onehot, sums, (((1,), (1,)), ((), ())), preferred_element_type=jnp.float32
            )
            value = value + jnp.pad(
                own[:, None, :], ((0, 0), (frames, 7), (0, right.shape[0] - frames))
            )
        return value

    partials = LogCode(0.0218, 6800.0 * pixels * cores, True)
    results = LogCode(1 / 140.0, 140.0, False)

    def reduce_owned(left, right, sums=None, exact=False):
        def part(owner_core, ks):
            return gram(onehot_of(owner_core, ks), left, right, sums)

        theirs = {}
        for name, ks in (("o", away_ks), ("x", own_ks)):
            if cores > 1 and len(ks):
                theirs[name] = swap_core(part(other, ks))
        total = None
        if across > 1:
            sent = part(core, away_ks)
            if cores > 1:
                sent = sent + theirs["o"]
            got = []
            for k in range(1, across):
                value = sent[(k - 1) * owned : k * owned]
                if not exact:
                    value = partials.encode(value)
                value = shift_x(value, k)
                got.append(value if exact else partials.decode(value))
            total = sum(got[1:], got[0])
        here = part(core, own_ks)
        if cores > 1:
            here = here + theirs["x"]
        here = lax.optimization_barrier(here)
        return here if total is None else here + total

    out = jnp.zeros((owned, frames, tm * frames), jnp.float32)

    def place(out, value, zs, ys):
        at = (zs % outer * inner + ys % inner) * frames
        return lax.dynamic_update_slice_in_dim(out, value, at, 2)

    ones = jnp.ones((8, pixels), jnp.bfloat16)
    extended = jnp.concatenate([intensity, ones], axis=0)
    total = reduce_owned(extended, extended, exact=True)
    row_sums = total[:, :frames, frames]
    scale = total[:, frames, frames][:, None, None] / row_sums[:, :, None]
    column_sums = [total[:, frames : frames + 1, :frames]]
    size = total[:, frames : frames + 1, frames : frames + 1]
    out = place(out, total[:, :frames, :frames] * scale / column_sums[0], z, y)
    group = jnp.concatenate(beside, axis=0)

    def beside_group(out):
        if inner == 1:
            return out
        total = reduce_owned(extended, group[frames:])
        for k in range(1, inner):
            part = total[:, :, (k - 1) * frames : k * frames]
            column_sums.append(part[:, frames : frames + 1])
            out = place(out, part[:, :frames] * scale / column_sums[k], z, y - k)
        return out

    def remote_group(s, out):
        left = jnp.concatenate([remote[s], jnp.zeros((8, pixels), jnp.bfloat16)], axis=0)
        total = reduce_owned(left, group, sums=remote[s])
        left_sums = jnp.transpose(total[:, frames : frames + 1, :frames], (0, 2, 1))
        value = total[:, :frames] * (size / left_sums) / jnp.concatenate(column_sums, axis=2)
        if 2 * s != outer:
            back = shift_z(results.encode(value), -s)
            back = results.decode(back)
            for k in range(inner):
                out = place(out, back[:, :, k * frames : (k + 1) * frames], z + s, y - k)
        for k in range(inner):
            block = jnp.transpose(value[:, :, k * frames : (k + 1) * frames], (0, 2, 1))
            if k > 0:
                block = results.decode(shift_y(results.encode(block), -k))
            out = place(out, block, z - s, y + k)
        return out

    out = beside_group(out)
    for s in range(1, half + 1):
        out = remote_group(s, out)
    return out


MESH = pl.DeviceIdType.MESH
TILE = 16
CHUNKS = 2


def fits_kernel(shape):
    inner = inner_extent(shape["tm"])
    return shape["tm"] // inner == 4 and inner == 2 and shape["pix"] == 4


def exchange(owned, partials, results, *refs):
    (counts, dead_time, flat_field, cycle_map,
     diagonal, pair, local, side_in, back_in,
     wide, right, ring, swap_out, swap_in, x_out, x_in, here, side_out, back_out,
     diag_out, diag_in, diag_x_out, diag_x_in, diag_here,
     pair_out, pair_in, pair_x_out, pair_x_in, pair_here,
     sums_out, sums_core, sums_chip, sums_x, scale_own, scale_side, scale_first, scale_second,
     columns, pair_columns,
     core_send, core_recv, x_send, x_recv, up_send, up_recv, back_send, back_recv,
     side_send, side_recv, diag_send, diag_recv, pair_send, pair_recv, sum_send, sum_recv) = refs
    frames, pixels = counts.shape
    step, last = frames // CHUNKS, 2 * CHUNKS - 1
    at_tm, at_pix = lax.axis_index("tm"), lax.axis_index("pix")
    z, y = at_tm // 2, at_tm % 2
    x, core = at_pix // 2, at_pix % 2
    to_y = {"tm": z * 2 + 1 - y}
    to_up = {"tm": (z + 1) % 4 * 2 + y}
    to_down = {"tm": (z + 3) % 4 * 2 + y}
    to_core = {"pix": x * 2 + 1 - core}
    to_x = {"pix": (1 - x) * 2 + core}
    own, beside, every = pl.ds(0, frames), pl.ds(frames, frames), pl.ds(0, 2 * frames)

    barrier = pltpu.get_barrier_semaphore()
    for target in (to_y, to_up, to_down, to_core, to_x):
        pl.semaphore_signal(barrier, inc=1, device_id=target, device_id_type=MESH)

    def correct(i, carry):
        rows = pl.ds(pl.multiple_of(i * TILE, TILE), TILE)
        raw = counts[rows, :]
        value = raw / (1.0 - dead_time[...] * raw) * flat_field[...]
        right[rows, :] = value.astype(jnp.bfloat16)
        return carry

    lax.fori_loop(0, frames // TILE, correct, 0)
    pl.semaphore_wait(barrier, 5)

    def remote(source, target, send, recv, device):
        return pltpu.make_async_remote_copy(
            src_ref=source, dst_ref=target, send_sem=send, recv_sem=recv,
            device_id=device, device_id_type=MESH,
        )

    copies = []

    def start(*args):
        copy = remote(*args)
        copy.start()
        copies.append(copy)
        return copy

    def chunk(n):
        return pl.ds(pl.multiple_of(n * step, step), step)

    by_side = start(right.at[own], right.at[beside], side_send.at[0], side_recv.at[0], to_y)
    for n in range(CHUNKS):
        start(right.at[chunk(n)], ring.at[chunk(n)], up_send.at[n], up_recv.at[n], to_up)

    def forward(n):
        copy = remote(ring.at[chunk(n)], ring.at[chunk(n + CHUNKS)],
                      up_send.at[n + CHUNKS], up_recv.at[n + CHUNKS], to_up)
        return copy

    def landed(n):
        remote(ring.at[chunk(n)], ring.at[chunk(n)], up_send.at[n], up_recv.at[n], to_up).wait_recv()

    ids = lax.broadcasted_iota(jnp.int32, (CYCLES, pixels), 0)
    onehot = jnp.where(jnp.broadcast_to(cycle_map[...], (CYCLES, pixels)) == ids, 1.0, 0.0)
    counted = lax.dot_general(
        onehot.astype(jnp.bfloat16), right[own, :], (((1,), (1,)), ((), ())),
        preferred_element_type=jnp.float32,
    )
    size = jnp.sum(onehot, axis=1, keepdims=True)
    sums_out[:, own] = counted
    sums_out[:, beside] = jnp.broadcast_to(size, counted.shape)
    by_core = start(sums_out, sums_core, sum_send.at[0], sum_recv.at[0], to_core)

    def fill(r, carry):
        hit = jnp.broadcast_to(cycle_map[...], (TILE, pixels)) == r
        wide[r] = jnp.where(hit, 1.0, 0.0).astype(jnp.bfloat16)
        return carry

    lax.fori_loop(0, CYCLES // 2, fill, 0)
    by_core.wait_recv()
    sums_chip[...] = sums_out[...] + sums_core[...]
    by_x = start(sums_chip, sums_x, sum_send.at[1], sum_recv.at[1], to_x)
    lax.fori_loop(CYCLES // 2, CYCLES, fill, 0)

    bases = [((1 - x) * 2 + 1 - core) * owned, (x * 2 + 1 - core) * owned,
             ((1 - x) * 2 + core) * owned, at_pix * owned]

    def reduce_unit(left, rows, count, cols, out, inn, code_out, code_in, kept, csem, xsem):
        def product(group):
            block = left[rows, :].reshape(count // TILE, TILE, pixels)
            masked = jnp.concatenate(
                [(block * wide[bases[group] + i][None]).reshape(count, pixels) for i in range(owned)],
                axis=0,
            )
            value = lax.dot_general(
                masked, right[cols, :], (((1,), (1,)), ((), ())), preferred_element_type=jnp.float32
            )
            return value.reshape(owned, count, cols.size)

        away = []
        for g in range(2):
            out[g] = product(g)
            copy = remote(out.at[g], inn.at[g], csem[0].at[g], csem[1].at[g], to_core)
            copy.start()
            away.append(copy)
        value = product(2)
        away[0].wait_recv()
        code_out[...] = partials.encode(value + inn[0])
        across = remote(code_out, code_in, xsem[0], xsem[1], to_x)
        across.start()
        value = product(3)
        away[1].wait_recv()
        kept[...] = value + inn[1]
        return [*away, across]

    def part(refs, n):
        return [ref.at[n] for ref in refs]

    diag_sems = (diag_send, diag_recv)
    sent = reduce_unit(right, own, frames, own, diag_out, diag_in, diag_x_out, diag_x_in, diag_here,
                       diag_sems, part(diag_sems, 2))
    copies += sent
    by_x.wait_recv()
    mine = pl.ds(pl.multiple_of(at_pix * owned, owned), owned)
    scale_own[...] = sums_chip[mine, :] + sums_x[mine, :]
    by_y = start(scale_own, scale_side, sum_send.at[2], sum_recv.at[2], to_y)
    by_up = start(scale_own, scale_first, sum_send.at[3], sum_recv.at[3], to_up)

    def pass_on(n):
        landed(n)
        copy = forward(n)
        copy.start()
        copies.append(copy)

    for n in range(CHUNKS - 1):
        pass_on(n)
    by_up.wait_recv()
    by_up2 = start(scale_first, scale_second, sum_send.at[4], sum_recv.at[4], to_up)
    size = scale_own[:, beside]
    own_sums = scale_own[:, own]
    own_columns = jnp.transpose(size / own_sums, (1, 0))
    sent[2].wait_recv()
    for r in range(owned):
        value = diag_here[r] + partials.decode(diag_x_in[r])
        diagonal[r] = value * own_columns[:, r : r + 1] * (1.0 / own_sums[r : r + 1])

    by_y.wait_recv()
    side_sums = scale_side[:, own]
    lower = y == 0
    pair_columns[...] = jnp.transpose(size / jnp.where(lower, own_sums, side_sums), (1, 0))
    pair_lanes = 1.0 / jnp.where(lower, side_sums, own_sums)
    lanes = 1.0 / jnp.concatenate([own_sums, side_sums], axis=1)
    columns[own, :] = jnp.transpose(size / scale_first[:, own], (1, 0))
    by_up2.wait_recv()
    columns[beside, :] = jnp.transpose(size / scale_second[:, own], (1, 0))

    by_side.wait_recv()
    pass_on(CHUNKS - 1)
    half = frames // 2
    half_rows = pl.ds(pl.multiple_of(y * half, half), half)
    pair_sems = (pair_send, pair_recv)
    sent = reduce_unit(right, pl.ds(pl.multiple_of(y * (frames + half), half), half), half,
                       pl.ds(pl.multiple_of((1 - y) * frames, frames), frames),
                       pair_out, pair_in, pair_x_out, pair_x_in, pair_here,
                       pair_sems, part(pair_sems, 2))
    copies += sent

    core_sems, x_sems = (core_send, core_recv), (x_send, x_recv)

    def unit(n):
        return reduce_unit(ring, chunk(n), step, every, swap_out.at[n], swap_in.at[n],
                           x_out.at[n], x_in.at[n], here.at[n], part(core_sems, n), part(x_sems, n))

    def to_side(n):
        return remote(side_out.at[n], side_in.at[:, chunk(n)],
                      side_send.at[1 + n], side_recv.at[1 + n], to_y)

    def to_back(n):
        return remote(back_out.at[n], back_in.at[:, chunk(n)], back_send.at[n], back_recv.at[n], to_down)

    def finish(n, back):
        remote(x_out.at[n], x_in.at[n], x_send.at[n], x_recv.at[n], to_x).wait_recv()
        for r in range(owned):
            value = here[n, r] + partials.decode(x_in[n, r])
            value = value * columns[chunk(n), r : r + 1] * lanes[r : r + 1]
            local[r, chunk(n), :] = value[:, :frames]
            code = results.encode(value)
            side_out[n, r] = code[:, frames:]
            if back:
                back_out[n, r] = code
        if back:
            to_back(n).start()
        to_side(n).start()

    copies += unit(0)
    sent[2].wait_recv()
    for r in range(owned):
        value = pair_here[r] + partials.decode(pair_x_in[r])
        value = value * pair_columns[half_rows, r : r + 1] * pair_lanes[r : r + 1]
        pair[r, half_rows, :] = results.encode(value)
    by_pair = start(pair.at[:, half_rows], pair.at[:, half_rows], pair_send.at[3], pair_recv.at[3], to_y)
    for n in range(1, 2 * CHUNKS):
        if n >= CHUNKS:
            landed(n)
        copies += unit(n)
        finish(n - 1, n - 1 < CHUNKS)
    finish(last, False)
    by_pair.wait_recv()
    for n in range(2 * CHUNKS):
        copies.append(to_side(n))
        copies[-1].wait_recv()
    for n in range(CHUNKS):
        copies.append(to_back(n))
        copies[-1].wait_recv()
    for copy in copies:
        copy.wait_send()


def assemble(results, diagonal, pair, local, side, back, out):
    frames = diagonal.shape[1]
    at_tm = lax.axis_index("tm")
    z, y = at_tm // 2, at_tm % 2

    def put(dz, dy, value):
        block = (z + dz + 4) % 4 * 2 + (y + dy) % 2
        out[0, :, pl.ds(pl.multiple_of(block * frames, frames), frames)] = value

    def turn(value):
        return jnp.transpose(value, (1, 0))

    put(0, 0, diagonal[0])
    value = results.decode(pair[0])
    put(0, 1, jnp.where(y == 0, value, turn(value)))
    for s in range(2):
        rows = pl.ds(s * frames, frames)
        put(-1 - s, 0, turn(local[0, rows, :]))
        put(-1 - s, 1, turn(results.decode(side[0, rows, :])))
    value = results.decode(back[0])
    put(1, 0, value[:, :frames])
    put(1, 1, value[:, frames:])


def per_device_kernel(counts, dead_time, flat_field, cycle_map):
    frames, pixels = counts.shape
    tm, pix = lax.axis_size("tm"), lax.axis_size("pix")
    owned = CYCLES // pix
    partials = LogCode(0.0218, 6800.0 * pixels * 2, True)
    results = LogCode(1 / 140.0, 140.0, False)
    f32, bf16, i16 = jnp.float32, jnp.bfloat16, jnp.int16
    vmem, dma = pltpu.VMEM, pltpu.SemaphoreType.DMA
    both, half, step, units = 2 * frames, frames // 2, frames // CHUNKS, 2 * CHUNKS
    small = (owned, both)
    scratch = [
        vmem((CYCLES, TILE, pixels), bf16),
        vmem((both, pixels), bf16),
        vmem((both, pixels), bf16),
        *[vmem((units, 2, owned, step, both), f32)] * 2,
        *[vmem((units, owned, step, both), i16)] * 2,
        vmem((units, owned, step, both), f32),
        vmem((units, owned, step, frames), i16),
        vmem((CHUNKS, owned, step, both), i16),
        *[vmem((2, owned, frames, frames), f32)] * 2,
        *[vmem((owned, frames, frames), i16)] * 2,
        vmem((owned, frames, frames), f32),
        *[vmem((2, owned, half, frames), f32)] * 2,
        *[vmem((owned, half, frames), i16)] * 2,
        vmem((owned, half, frames), f32),
        *[vmem((CYCLES, both), f32)] * 4,
        *[vmem(small, f32)] * 4,
        vmem((both, owned), f32),
        vmem((frames, owned), f32),
        dma((units, 2)), dma((units, 2)), dma((units,)), dma((units,)),
        dma((units,)), dma((units,)), dma((CHUNKS,)), dma((CHUNKS,)),
        dma((1 + units,)), dma((1 + units,)), dma((3,)), dma((3,)), dma((4,)), dma((4,)),
        dma((5,)), dma((5,)),
    ]
    shapes = [
        ((owned, frames, frames), f32), ((owned, frames, frames), i16),
        ((owned, both, frames), f32), ((owned, both, frames), i16), ((owned, frames, both), i16),
    ]
    pieces = pl.pallas_call(
        functools.partial(exchange, owned, partials, results),
        out_shape=[jax.ShapeDtypeStruct(*shape) for shape in shapes],
        in_specs=[pl.BlockSpec(memory_space=pltpu.VMEM)] * 4,
        out_specs=[pl.BlockSpec(memory_space=pltpu.VMEM)] * 5,
        scratch_shapes=scratch,
        compiler_params=pltpu.CompilerParams(
            collective_id=0, has_side_effects=True, vmem_limit_bytes=60 << 20
        ),
    )(counts, dead_time[None, :], flat_field[None, :], cycle_map[None, :])
    return pl.pallas_call(
        functools.partial(assemble, results),
        grid=(owned,),
        out_shape=jax.ShapeDtypeStruct((owned, frames, tm * frames), f32),
        in_specs=[pl.BlockSpec((1, *shape[1:]), lambda r: (r, 0, 0)) for shape, _ in shapes],
        out_specs=pl.BlockSpec((1, frames, tm * frames), lambda r: (r, 0, 0)),
    )(*pieces)


def solution(mesh):
    kernel_path = fits_kernel(mesh.shape)
    device_program = per_device_kernel if kernel_path else per_device
    placed = (P("tm", "pix"), P("pix"), P("pix"), P("pix"))

    return jax.shard_map(
        device_program, mesh=mesh, in_specs=placed, out_specs=P("pix", "tm", None), check_vma=False
    )
```

profile of v0, /device:TPU:0, one launch (start us, length us, event | category | flops | bytes accessed | tf_op | source)
XLA Modules:
  0.0 108.1 jit_solution(9918008213235754555)
XLA Ops:
  0.0 101.1 %shard_map.46 = (f32[8,128,128]{2,1,0:T(8,128)}, s16[8,128,128]{2,1,0:T(8,128)(2,1)}, f32[8,256,128]{2,1,0:T(8,128)}, s16[8,256,128]{2,1,0:T(8,128)(2,1)}, s16[8,128,256]{2,1,0:T(8,128)(2,1)}) custom-call(f32[128,4096]{1,0:T(8,128)} %refs_0_.1, f32[1,4096]{1,0:T(1,128)} %bitcast.3, f32[1,4096]{1,0:T(1,128)} %bitcast.4, s32[1,4096]{1,0:T(1,128)} %bitcast.5), custom_call_target="tpu_custom_call" | custom-call | tf_op jit(solution)/shard_map/pallas_call | solution.py:477
  101.1 7.0 %shard_map.47 = f32[8,128,1024]{2,1,0:T(8,128)} custom-call(f32[8,128,128]{2,1,0:T(8,128)} %get-tuple-element.10.diagonal, s16[8,128,128]{2,1,0:T(8,128)(2,1)} %get-tuple-element.11.pair, f32[8,256,128]{2,1,0:T(8,128)} %get-tuple-element.12.local, s16[8,256,128]{2,1,0:T(8,128)(2,1)} %get-tuple-element.13.side, s16[8,128,256]{2,1,0:T(8,128)(2,1)} %get-tuple-element.14.back), custom_call_target="tpu_custom_call" | custom-call | tf_op jit(solution)/shard_map/pallas_call | solution.py:487
where the time goes:
time: 108 us
  Pallas kernels  108 us (100%)
    pallas_call x1, Pallas kernels, per_device_kernel(): pl.pallas_call(functools.partial(exchange, owned, partials, results), out...  101 us
    pallas_call x1, Pallas kernels, per_device_kernel(): pl.pallas_call(functools.partial(assemble, results), grid=(owned,), out_s...  7 us

commit v1 on v0

--- a/solution.py
+++ b/solution.py
@@ -198,7 +198,7 @@
      diag_out, diag_in, diag_x_out, diag_x_in, diag_here,
      pair_out, pair_in, pair_x_out, pair_x_in, pair_here,
      sums_out, sums_core, sums_chip, sums_x, scale_own, scale_side, scale_first, scale_second,
-     columns, pair_columns,
+     columns, pair_columns, lanes,
      core_send, core_recv, x_send, x_recv, up_send, up_recv, back_send, back_recv,
      side_send, side_recv, diag_send, diag_recv, pair_send, pair_recv, sum_send, sum_recv) = refs
     frames, pixels = counts.shape
@@ -245,16 +245,16 @@
         return pl.ds(pl.multiple_of(n * step, step), step)
 
     by_side = start(right.at[own], right.at[beside], side_send.at[0], side_recv.at[0], to_y)
-    for n in range(CHUNKS):
-        start(right.at[chunk(n)], ring.at[chunk(n)], up_send.at[n], up_recv.at[n], to_up)
+
+    def to_ring(n):
+        return remote(right.at[chunk(n)], ring.at[chunk(n)], up_send.at[n], up_recv.at[n], to_up)
 
     def forward(n):
-        copy = remote(ring.at[chunk(n)], ring.at[chunk(n + CHUNKS)],
+        return remote(ring.at[chunk(n)], ring.at[chunk(n + CHUNKS)],
                       up_send.at[n + CHUNKS], up_recv.at[n + CHUNKS], to_up)
-        return copy
-
-    def landed(n):
-        remote(ring.at[chunk(n)], ring.at[chunk(n)], up_send.at[n], up_recv.at[n], to_up).wait_recv()
+
+    copies += [to_ring(n) for n in range(CHUNKS)] + [forward(n) for n in range(CHUNKS)]
+    to_ring(0).start()
 
     ids = lax.broadcasted_iota(jnp.int32, (CYCLES, pixels), 0)
     onehot = jnp.where(jnp.broadcast_to(cycle_map[...], (CYCLES, pixels)) == ids, 1.0, 0.0)
@@ -277,137 +277,171 @@
     sums_chip[...] = sums_out[...] + sums_core[...]
     by_x = start(sums_chip, sums_x, sum_send.at[1], sum_recv.at[1], to_x)
     lax.fori_loop(CYCLES // 2, CYCLES, fill, 0)
-
-    bases = [((1 - x) * 2 + 1 - core) * owned, (x * 2 + 1 - core) * owned,
-             ((1 - x) * 2 + core) * owned, at_pix * owned]
-
-    def reduce_unit(left, rows, count, cols, out, inn, code_out, code_in, kept, csem, xsem):
-        def product(group):
+    by_x.wait_recv()
+    mine = pl.ds(pl.multiple_of(at_pix * owned, owned), owned)
+    scale_own[...] = sums_chip[mine, :] + sums_x[mine, :]
+    by_y = start(scale_own, scale_side, sum_send.at[2], sum_recv.at[2], to_y)
+    by_up = start(scale_own, scale_first, sum_send.at[3], sum_recv.at[3], to_up)
+    for n in range(1, CHUNKS):
+        to_ring(n).start()
+
+    away_base, own_base = (1 - x) * 2 * owned, x * 2 * owned
+
+    def reduce_unit(left, rows, count, cols, made, to_other, inn, code_out, to_across, kept):
+        def product(j, carry):
+            owner_core = lax.rem(core + 1 + j, 2)
             block = left[rows, :].reshape(count // TILE, TILE, pixels)
             masked = jnp.concatenate(
-                [(block * wide[bases[group] + i][None]).reshape(count, pixels) for i in range(owned)],
+                [
+                    (block * wide[base + owner_core * owned + i][None]).reshape(count, pixels)
+                    for base in (away_base, own_base)
+                    for i in range(owned)
+                ],
                 axis=0,
             )
             value = lax.dot_general(
                 masked, right[cols, :], (((1,), (1,)), ((), ())), preferred_element_type=jnp.float32
             )
-            return value.reshape(owned, count, cols.size)
-
-        away = []
-        for g in range(2):
-            out[g] = product(g)
-            copy = remote(out.at[g], inn.at[g], csem[0].at[g], csem[1].at[g], to_core)
-            copy.start()
-            away.append(copy)
-        value = product(2)
-        away[0].wait_recv()
-        code_out[...] = partials.encode(value + inn[0])
-        across = remote(code_out, code_in, xsem[0], xsem[1], to_x)
-        across.start()
-        value = product(3)
-        away[1].wait_recv()
-        kept[...] = value + inn[1]
-        return [*away, across]
-
-    def part(refs, n):
-        return [ref.at[n] for ref in refs]
-
-    diag_sems = (diag_send, diag_recv)
-    sent = reduce_unit(right, own, frames, own, diag_out, diag_in, diag_x_out, diag_x_in, diag_here,
-                       diag_sems, part(diag_sems, 2))
-    copies += sent
-    by_x.wait_recv()
-    mine = pl.ds(pl.multiple_of(at_pix * owned, owned), owned)
-    scale_own[...] = sums_chip[mine, :] + sums_x[mine, :]
-    by_y = start(scale_own, scale_side, sum_send.at[2], sum_recv.at[2], to_y)
-    by_up = start(scale_own, scale_first, sum_send.at[3], sum_recv.at[3], to_up)
+            made[j] = value.reshape(2, owned, count, cols.size)
+
+            @pl.when(j == 0)
+            def _():
+                to_other.start()
+
+            return carry
+
+        lax.fori_loop(0, 2, product, 0)
+        to_other.wait_recv()
+        code_out[...] = partials.encode(made[1, 0] + inn[0])
+        to_across.start()
+        kept[...] = made[1, 1] + inn[1]
+
+    half = frames // 2
+
+    def diag_core(n):
+        return remote(diag_out.at[n, 0], diag_in.at[n], diag_send.at[n], diag_recv.at[n], to_core)
+
+    def diag_across(n):
+        return remote(diag_x_out.at[n], diag_x_in.at[n],
+                      diag_send.at[2 + n], diag_recv.at[2 + n], to_x)
+
+    def diag_unit(n, carry):
+        rows = pl.ds(pl.multiple_of(n * half, half), half)
+        reduce_unit(right, rows, half, own, diag_out.at[n], diag_core(n), diag_in.at[n],
+                    diag_x_out.at[n], diag_across(n), diag_here.at[n])
+        return carry
+
+    lax.fori_loop(0, 2, diag_unit, 0)
+    copies += [diag_core(0), diag_core(1), diag_across(0), diag_across(1)]
 
     def pass_on(n):
-        landed(n)
-        copy = forward(n)
-        copy.start()
-        copies.append(copy)
-
+        remote(ring.at[chunk(n)], ring.at[chunk(n)], up_send.at[n], up_recv.at[n], to_up).wait_recv()
+        forward(n).start()
+
+    by_up.wait_recv()
+    by_up2 = start(scale_first, scale_second, sum_send.at[4], sum_recv.at[4], to_up)
     for n in range(CHUNKS - 1):
         pass_on(n)
-    by_up.wait_recv()
-    by_up2 = start(scale_first, scale_second, sum_send.at[4], sum_recv.at[4], to_up)
     size = scale_own[:, beside]
     own_sums = scale_own[:, own]
     own_columns = jnp.transpose(size / own_sums, (1, 0))
-    sent[2].wait_recv()
-    for r in range(owned):
-        value = diag_here[r] + partials.decode(diag_x_in[r])
-        diagonal[r] = value * own_columns[:, r : r + 1] * (1.0 / own_sums[r : r + 1])
+    columns[own, :] = jnp.transpose(size / scale_first[:, own], (1, 0))
+    for n in range(2):
+        rows = pl.ds(n * half, half)
+        diag_across(n).wait_recv()
+        for r in range(owned):
+            value = diag_here[n, r] + partials.decode(diag_x_in[n, r])
+            value = value * own_columns[n * half : (n + 1) * half, r : r + 1]
+            diagonal[r, rows, :] = value * (1.0 / own_sums[r : r + 1])
+
+    by_side.wait_recv()
+    pass_on(CHUNKS - 1)
+    half_rows = pl.ds(pl.multiple_of(y * half, half), half)
+    pair_core = remote(pair_out.at[0], pair_in, pair_send.at[0], pair_recv.at[0], to_core)
+    pair_across = remote(pair_x_out, pair_x_in, pair_send.at[1], pair_recv.at[1], to_x)
+    reduce_unit(right, pl.ds(pl.multiple_of(y * (frames + half), half), half), half,
+                pl.ds(pl.multiple_of((1 - y) * frames, frames), frames),
+                pair_out, pair_core, pair_in, pair_x_out, pair_across, pair_here)
+    copies += [pair_core, pair_across]
 
     by_y.wait_recv()
     side_sums = scale_side[:, own]
     lower = y == 0
     pair_columns[...] = jnp.transpose(size / jnp.where(lower, own_sums, side_sums), (1, 0))
     pair_lanes = 1.0 / jnp.where(lower, side_sums, own_sums)
-    lanes = 1.0 / jnp.concatenate([own_sums, side_sums], axis=1)
-    columns[own, :] = jnp.transpose(size / scale_first[:, own], (1, 0))
-    by_up2.wait_recv()
-    columns[beside, :] = jnp.transpose(size / scale_second[:, own], (1, 0))
-
-    by_side.wait_recv()
-    pass_on(CHUNKS - 1)
-    half = frames // 2
-    half_rows = pl.ds(pl.multiple_of(y * half, half), half)
-    pair_sems = (pair_send, pair_recv)
-    sent = reduce_unit(right, pl.ds(pl.multiple_of(y * (frames + half), half), half), half,
-                       pl.ds(pl.multiple_of((1 - y) * frames, frames), frames),
-                       pair_out, pair_in, pair_x_out, pair_x_in, pair_here,
-                       pair_sems, part(pair_sems, 2))
-    copies += sent
-
-    core_sems, x_sems = (core_send, core_recv), (x_send, x_recv)
-
-    def unit(n):
-        return reduce_unit(ring, chunk(n), step, every, swap_out.at[n], swap_in.at[n],
-                           x_out.at[n], x_in.at[n], here.at[n], part(core_sems, n), part(x_sems, n))
+    lanes[...] = 1.0 / jnp.concatenate([own_sums, side_sums], axis=1)
+
+    def to_other(n):
+        return remote(swap_out.at[n, 0], swap_in.at[n], core_send.at[n], core_recv.at[n], to_core)
+
+    def to_across(n):
+        return remote(x_out.at[n], x_in.at[n], x_send.at[n], x_recv.at[n], to_x)
 
     def to_side(n):
-        return remote(side_out.at[n], side_in.at[:, chunk(n)],
-                      side_send.at[1 + n], side_recv.at[1 + n], to_y)
+        return remote(side_out.at[n], side_in.at[n], side_send.at[1 + n], side_recv.at[1 + n], to_y)
 
     def to_back(n):
         return remote(back_out.at[n], back_in.at[:, chunk(n)], back_send.at[n], back_recv.at[n], to_down)
 
-    def finish(n, back):
-        remote(x_out.at[n], x_in.at[n], x_send.at[n], x_recv.at[n], to_x).wait_recv()
+    by_pair = remote(pair.at[:, half_rows], pair.at[:, half_rows],
+                     pair_send.at[2], pair_recv.at[2], to_y)
+
+    def finish(n):
+        to_across(n).wait_recv()
+
         for r in range(owned):
             value = here[n, r] + partials.decode(x_in[n, r])
-            value = value * columns[chunk(n), r : r + 1] * lanes[r : r + 1]
-            local[r, chunk(n), :] = value[:, :frames]
-            code = results.encode(value)
-            side_out[n, r] = code[:, frames:]
-            if back:
-                back_out[n, r] = code
-        if back:
+            value = value * columns[chunk(n), r : r + 1] * lanes[r : r + 1, :]
+            back_out[n, r] = results.encode(value)
+            turned = jnp.transpose(value, (1, 0))
+            side_out[n, r] = results.encode(turned[frames:])
+            local[n, r] = turned[:frames]
+
+        @pl.when(n < CHUNKS)
+        def _():
             to_back(n).start()
+
         to_side(n).start()
 
-    copies += unit(0)
-    sent[2].wait_recv()
-    for r in range(owned):
-        value = pair_here[r] + partials.decode(pair_x_in[r])
-        value = value * pair_columns[half_rows, r : r + 1] * pair_lanes[r : r + 1]
-        pair[r, half_rows, :] = results.encode(value)
-    by_pair = start(pair.at[:, half_rows], pair.at[:, half_rows], pair_send.at[3], pair_recv.at[3], to_y)
-    for n in range(1, 2 * CHUNKS):
-        if n >= CHUNKS:
-            landed(n)
-        copies += unit(n)
-        finish(n - 1, n - 1 < CHUNKS)
-    finish(last, False)
+    def unit(n, carry):
+        @pl.when(n >= CHUNKS)
+        def _():
+            remote(ring.at[chunk(n)], ring.at[chunk(n)],
+                   up_send.at[n], up_recv.at[n], to_up).wait_recv()
+
+        reduce_unit(ring, chunk(n), step, every, swap_out.at[n], to_other(n), swap_in.at[n],
+                    x_out.at[n], to_across(n), here.at[n])
+
+        @pl.when(n == 0)
+        def _():
+            pair_across.wait_recv()
+            for r in range(owned):
+                value = pair_here[r] + partials.decode(pair_x_in[r])
+                value = value * pair_columns[half_rows, r : r + 1] * pair_lanes[r : r + 1]
+                pair[r, half_rows, :] = results.encode(value)
+            by_pair.start()
+
+        @pl.when(n == 1)
+        def _():
+            by_up2.wait_recv()
+            columns[beside, :] = jnp.transpose(size / scale_second[:, own], (1, 0))
+
+        @pl.when(n > 0)
+        def _():
+            finish(n - 1)
+
+        return carry
+
+    lax.fori_loop(0, 2 * CHUNKS, unit, 0)
+    finish(jnp.int32(last))
     by_pair.wait_recv()
+    copies.append(by_pair)
     for n in range(2 * CHUNKS):
-        copies.append(to_side(n))
-        copies[-1].wait_recv()
+        copies += [to_other(n), to_across(n), to_side(n)]
+        to_side(n).wait_recv()
     for n in range(CHUNKS):
         copies.append(to_back(n))
-        copies[-1].wait_recv()
+        to_back(n).wait_recv()
     for copy in copies:
         copy.wait_send()
 
@@ -425,12 +459,19 @@
         return jnp.transpose(value, (1, 0))
 
     put(0, 0, diagonal[0])
-    value = results.decode(pair[0])
-    put(0, 1, jnp.where(y == 0, value, turn(value)))
+
+    @pl.when(y == 0)
+    def _():
+        put(0, 1, results.decode(pair[0]))
+
+    @pl.when(y == 1)
+    def _():
+        put(0, 1, turn(results.decode(pair[0])))
+
     for s in range(2):
-        rows = pl.ds(s * frames, frames)
-        put(-1 - s, 0, turn(local[0, rows, :]))
-        put(-1 - s, 1, turn(results.decode(side[0, rows, :])))
+        chunks = range(s * CHUNKS, (s + 1) * CHUNKS)
+        put(-1 - s, 0, jnp.concatenate([local[n, 0] for n in chunks], axis=1))
+        put(-1 - s, 1, results.decode(jnp.concatenate([side[n, 0] for n in chunks], axis=1)))
     value = results.decode(back[0])
     put(1, 0, value[:, :frames])
     put(1, 1, value[:, frames:])
@@ -450,29 +491,34 @@
         vmem((CYCLES, TILE, pixels), bf16),
         vmem((both, pixels), bf16),
         vmem((both, pixels), bf16),
-        *[vmem((units, 2, owned, step, both), f32)] * 2,
+        vmem((units, 2, 2, owned, step, both), f32),
+        vmem((units, 2, owned, step, both), f32),
         *[vmem((units, owned, step, both), i16)] * 2,
         vmem((units, owned, step, both), f32),
-        vmem((units, owned, step, frames), i16),
-        vmem((CHUNKS, owned, step, both), i16),
-        *[vmem((2, owned, frames, frames), f32)] * 2,
-        *[vmem((owned, frames, frames), i16)] * 2,
-        vmem((owned, frames, frames), f32),
-        *[vmem((2, owned, half, frames), f32)] * 2,
+        vmem((units, owned, frames, step), i16),
+        vmem((units, owned, step, both), i16),
+        vmem((2, 2, 2, owned, half, frames), f32),
+        vmem((2, 2, owned, half, frames), f32),
+        *[vmem((2, owned, half, frames), i16)] * 2,
+        vmem((2, owned, half, frames), f32),
+        vmem((2, 2, owned, half, frames), f32),
+        vmem((2, owned, half, frames), f32),
         *[vmem((owned, half, frames), i16)] * 2,
         vmem((owned, half, frames), f32),
         *[vmem((CYCLES, both), f32)] * 4,
         *[vmem(small, f32)] * 4,
         vmem((both, owned), f32),
         vmem((frames, owned), f32),
-        dma((units, 2)), dma((units, 2)), dma((units,)), dma((units,)),
+        vmem(small, f32),
+        dma((units,)), dma((units,)), dma((units,)), dma((units,)),
         dma((units,)), dma((units,)), dma((CHUNKS,)), dma((CHUNKS,)),
-        dma((1 + units,)), dma((1 + units,)), dma((3,)), dma((3,)), dma((4,)), dma((4,)),
+        dma((1 + units,)), dma((1 + units,)), dma((4,)), dma((4,)), dma((3,)), dma((3,)),
         dma((5,)), dma((5,)),
     ]
     shapes = [
         ((owned, frames, frames), f32), ((owned, frames, frames), i16),
-        ((owned, both, frames), f32), ((owned, both, frames), i16), ((owned, frames, both), i16),
+        ((units, owned, frames, step), f32), ((units, owned, frames, step), i16),
+        ((owned, frames, both), i16),
     ]
     pieces = pl.pallas_call(
         functools.partial(exchange, owned, partials, results),
@@ -488,7 +534,12 @@
         functools.partial(assemble, results),
         grid=(owned,),
         out_shape=jax.ShapeDtypeStruct((owned, frames, tm * frames), f32),
-        in_specs=[pl.BlockSpec((1, *shape[1:]), lambda r: (r, 0, 0)) for shape, _ in shapes],
+        in_specs=[
+            pl.BlockSpec((1, *shape[1:]), lambda r: (r, 0, 0))
+            if len(shape) == 3
+            else pl.BlockSpec((shape[0], 1, *shape[2:]), lambda r: (0, r, 0, 0))
+            for shape, _ in shapes
+        ],
         out_specs=pl.BlockSpec((1, frames, tm * frames), lambda r: (r, 0, 0)),
     )(*pieces)
 

time: 108 us -> 87.4 us (0.81)
  Pallas kernels: 108 us -> 87.1 us
    pallas_call x1, Pallas kernels: 101 us -> 80 us  [per_device_kernel(): pl.pallas_call(functools.partial(exchange, owned, partials, results), out...]
where the time goes in v1:
time: 87.4 us; the launch traced here: 87.1 us
  Pallas kernels  87.1 us (100%)
    pallas_call x1, Pallas kernels, per_device_kernel(): pl.pallas_call(functools.partial(exchange, owned, partials, results), out...  80 us
    pallas_call x1, Pallas kernels, per_device_kernel(): pl.pallas_call(functools.partial(assemble, results), grid=(owned,), out_s...  7.05 us

profile of v1, /device:TPU:0, one launch (start us, length us, event | category | flops | bytes accessed | tf_op | source)
XLA Modules:
  0.0 87.1 jit_solution(13261708530617707646)
XLA Ops:
  0.0 80.0 %shard_map.46 = (f32[8,128,128]{2,1,0:T(8,128)}, s16[8,128,128]{2,1,0:T(8,128)(2,1)}, f32[4,8,128,64]{3,2,1,0:T(8,128)}, s16[4,8,128,64]{3,2,1,0:T(8,128)(2,1)}, s16[8,128,256]{2,1,0:T(8,128)(2,1)}) custom-call(f32[128,4096]{1,0:T(8,128)} %refs_0_.1, f32[1,4096]{1,0:T(1,128)} %bitcast.3, f32[1,4096]{1,0:T(1,128)} %bitcast.4, s32[1,4096]{1,0:T(1,128)} %bitcast.5), custom_call_target="tpu_custom_call" | custom-call | tf_op jit(solution)/shard_map/pallas_call | solution.py:523
  80.1 7.0 %shard_map.47 = f32[8,128,1024]{2,1,0:T(8,128)} custom-call(f32[8,128,128]{2,1,0:T(8,128)} %get-tuple-element.10.diagonal, s16[8,128,128]{2,1,0:T(8,128)(2,1)} %get-tuple-element.11.pair, f32[4,8,128,64]{3,2,1,0:T(8,128)} %get-tuple-element.12.local, s16[4,8,128,64]{3,2,1,0:T(8,128)(2,1)} %get-tuple-element.13.side, s16[8,128,256]{2,1,0:T(8,128)(2,1)} %get-tuple-element.14.back), custom_call_target="tpu_custom_call" | custom-call | tf_op jit(solution)/shard_map/pallas_call | solution.py:533

commit v2 on v1

--- a/solution.py
+++ b/solution.py
@@ -193,14 +193,14 @@
 
 def exchange(owned, partials, results, *refs):
     (counts, dead_time, flat_field, cycle_map,
-     diagonal, pair, local, side_in, back_in,
+     diagonal, pair, local, side_in, back_in, diag_rows, pair_rows, local_rows, local_turned,
      wide, right, ring, swap_out, swap_in, x_out, x_in, here, side_out, back_out,
      diag_out, diag_in, diag_x_out, diag_x_in, diag_here,
      pair_out, pair_in, pair_x_out, pair_x_in, pair_here,
      sums_out, sums_core, sums_chip, sums_x, scale_own, scale_side, scale_first, scale_second,
      columns, pair_columns, lanes,
      core_send, core_recv, x_send, x_recv, up_send, up_recv, back_send, back_recv,
-     side_send, side_recv, diag_send, diag_recv, pair_send, pair_recv, sum_send, sum_recv) = refs
+     side_send, side_recv, diag_send, diag_recv, pair_send, pair_recv, sum_send, sum_recv, keep_sem) = refs
     frames, pixels = counts.shape
     step, last = frames // CHUNKS, 2 * CHUNKS - 1
     at_tm, at_pix = lax.axis_index("tm"), lax.axis_index("pix")
@@ -318,6 +318,9 @@
 
     half = frames // 2
 
+    def keep(source, target, n):
+        return pltpu.make_async_copy(source, target, keep_sem.at[n])
+
     def diag_core(n):
         return remote(diag_out.at[n, 0], diag_in.at[n], diag_send.at[n], diag_recv.at[n], to_core)
 
@@ -352,7 +355,8 @@
         for r in range(owned):
             value = diag_here[n, r] + partials.decode(diag_x_in[n, r])
             value = value * own_columns[n * half : (n + 1) * half, r : r + 1]
-            diagonal[r, rows, :] = value * (1.0 / own_sums[r : r + 1])
+            diag_rows[r, rows, :] = value * (1.0 / own_sums[r : r + 1])
+    keep(diag_rows, diagonal, 0).start()
 
     by_side.wait_recv()
     pass_on(CHUNKS - 1)
@@ -378,13 +382,12 @@
         return remote(x_out.at[n], x_in.at[n], x_send.at[n], x_recv.at[n], to_x)
 
     def to_side(n):
-        return remote(side_out.at[n], side_in.at[n], side_send.at[1 + n], side_recv.at[1 + n], to_y)
+        return remote(side_out.at[n], side_in.at[:, chunk(n)], side_send.at[1 + n], side_recv.at[1 + n], to_y)
 
     def to_back(n):
         return remote(back_out.at[n], back_in.at[:, chunk(n)], back_send.at[n], back_recv.at[n], to_down)
 
-    by_pair = remote(pair.at[:, half_rows], pair.at[:, half_rows],
-                     pair_send.at[2], pair_recv.at[2], to_y)
+    by_pair = remote(pair_rows, pair.at[:, half_rows], pair_send.at[2], pair_recv.at[2], to_y)
 
     def finish(n):
         to_across(n).wait_recv()
@@ -393,15 +396,19 @@
             value = here[n, r] + partials.decode(x_in[n, r])
             value = value * columns[chunk(n), r : r + 1] * lanes[r : r + 1, :]
             back_out[n, r] = results.encode(value)
-            turned = jnp.transpose(value, (1, 0))
-            side_out[n, r] = results.encode(turned[frames:])
-            local[n, r] = turned[:frames]
+            side_out[n, r] = results.encode(value[:, frames:])
+            local_rows[r, chunk(n), :] = value[:, :frames]
 
         @pl.when(n < CHUNKS)
         def _():
             to_back(n).start()
 
         to_side(n).start()
+
+    def turn(s):
+        for r in range(owned):
+            local_turned[s, r] = jnp.transpose(local_rows[r, pl.ds(s * frames, frames), :], (1, 0))
+        keep(local_turned.at[s], local.at[s], 1 + s).start()
 
     def unit(n, carry):
         @pl.when(n >= CHUNKS)
@@ -418,8 +425,9 @@
             for r in range(owned):
                 value = pair_here[r] + partials.decode(pair_x_in[r])
                 value = value * pair_columns[half_rows, r : r + 1] * pair_lanes[r : r + 1]
-                pair[r, half_rows, :] = results.encode(value)
+                pair_rows[r] = results.encode(value)
             by_pair.start()
+            keep(pair_rows, pair.at[:, half_rows], 3).start()
 
         @pl.when(n == 1)
         def _():
@@ -430,10 +438,15 @@
         def _():
             finish(n - 1)
 
+        @pl.when(n == CHUNKS)
+        def _():
+            turn(0)
+
         return carry
 
     lax.fori_loop(0, 2 * CHUNKS, unit, 0)
     finish(jnp.int32(last))
+    turn(1)
     by_pair.wait_recv()
     copies.append(by_pair)
     for n in range(2 * CHUNKS):
@@ -442,6 +455,10 @@
     for n in range(CHUNKS):
         copies.append(to_back(n))
         to_back(n).wait_recv()
+    keep(diag_rows, diagonal, 0).wait()
+    for s in range(2):
+        keep(local_turned.at[s], local.at[s], 1 + s).wait()
+    keep(pair_rows, pair.at[:, half_rows], 3).wait()
     for copy in copies:
         copy.wait_send()
 
@@ -469,9 +486,8 @@
         put(0, 1, turn(results.decode(pair[0])))
 
     for s in range(2):
-        chunks = range(s * CHUNKS, (s + 1) * CHUNKS)
-        put(-1 - s, 0, jnp.concatenate([local[n, 0] for n in chunks], axis=1))
-        put(-1 - s, 1, results.decode(jnp.concatenate([side[n, 0] for n in chunks], axis=1)))
+        put(-1 - s, 0, local[s, 0])
+        put(-1 - s, 1, turn(results.decode(side[0, pl.ds(s * frames, frames), :])))
     value = results.decode(back[0])
     put(1, 0, value[:, :frames])
     put(1, 1, value[:, frames:])
@@ -488,6 +504,10 @@
     both, half, step, units = 2 * frames, frames // 2, frames // CHUNKS, 2 * CHUNKS
     small = (owned, both)
     scratch = [
+        vmem((owned, frames, frames), f32),
+        vmem((owned, half, frames), i16),
+        vmem((owned, both, frames), f32),
+        vmem((2, owned, frames, frames), f32),
         vmem((CYCLES, TILE, pixels), bf16),
         vmem((both, pixels), bf16),
         vmem((both, pixels), bf16),
@@ -495,7 +515,7 @@
         vmem((units, 2, owned, step, both), f32),
         *[vmem((units, owned, step, both), i16)] * 2,
         vmem((units, owned, step, both), f32),
-        vmem((units, owned, frames, step), i16),
+        vmem((units, owned, step, frames), i16),
         vmem((units, owned, step, both), i16),
         vmem((2, 2, 2, owned, half, frames), f32),
         vmem((2, 2, owned, half, frames), f32),
@@ -513,18 +533,17 @@
         dma((units,)), dma((units,)), dma((units,)), dma((units,)),
         dma((units,)), dma((units,)), dma((CHUNKS,)), dma((CHUNKS,)),
         dma((1 + units,)), dma((1 + units,)), dma((4,)), dma((4,)), dma((3,)), dma((3,)),
-        dma((5,)), dma((5,)),
+        dma((5,)), dma((5,)), dma((4,)),
     ]
     shapes = [
         ((owned, frames, frames), f32), ((owned, frames, frames), i16),
-        ((units, owned, frames, step), f32), ((units, owned, frames, step), i16),
-        ((owned, frames, both), i16),
+        ((2, owned, frames, frames), f32), ((owned, both, frames), i16), ((owned, frames, both), i16),
     ]
     pieces = pl.pallas_call(
         functools.partial(exchange, owned, partials, results),
         out_shape=[jax.ShapeDtypeStruct(*shape) for shape in shapes],
         in_specs=[pl.BlockSpec(memory_space=pltpu.VMEM)] * 4,
-        out_specs=[pl.BlockSpec(memory_space=pltpu.VMEM)] * 5,
+        out_specs=[pl.BlockSpec(memory_space=pl.ANY)] * 5,
         scratch_shapes=scratch,
         compiler_params=pltpu.CompilerParams(
             collective_id=0, has_side_effects=True, vmem_limit_bytes=60 << 20

time: 87.4 us -> 82 us (0.938)
  Pallas kernels: 87.1 us -> 81.7 us
    pallas_call x1, Pallas kernels: 80 us -> 74.9 us  [per_device_kernel(): pl.pallas_call(functools.partial(exchange, owned, partials, results), out...]
where the time goes in v2:
time: 82 us; the launch traced here: 81.7 us
  Pallas kernels  81.7 us (100%)
    pallas_call x1, Pallas kernels, per_device_kernel(): pl.pallas_call(functools.partial(exchange, owned, partials, results), out...  74.9 us
    pallas_call x1, Pallas kernels, per_device_kernel(): pl.pallas_call(functools.partial(assemble, results), grid=(owned,), out_s...  6.81 us

profile of v2, /device:TPU:0, one launch (start us, length us, event | category | flops | bytes accessed | tf_op | source)
XLA Modules:
  0.0 81.7 jit_solution(5170084872837988045)
XLA Ops:
  0.0 74.9 %shard_map.46 = (f32[8,128,128]{2,1,0:T(8,128)}, s16[8,128,128]{2,1,0:T(8,128)(2,1)}, f32[2,8,128,128]{3,2,1,0:T(8,128)}, s16[8,256,128]{2,1,0:T(8,128)(2,1)}, s16[8,128,256]{2,1,0:T(8,128)(2,1)}) custom-call(f32[128,4096]{1,0:T(8,128)} %refs_0_.1, f32[1,4096]{1,0:T(1,128)} %bitcast.3, f32[1,4096]{1,0:T(1,128)} %bitcast.4, s32[1,4096]{1,0:T(1,128)} %bitcast.5), custom_call_target="tpu_custom_call" | custom-call | tf_op jit(solution)/shard_map/pallas_call | solution.py:542
  74.9 6.8 %shard_map.47 = f32[8,128,1024]{2,1,0:T(8,128)} custom-call(f32[8,128,128]{2,1,0:T(8,128)} %get-tuple-element.10.diagonal, s16[8,128,128]{2,1,0:T(8,128)(2,1)} %get-tuple-element.11.pair, f32[2,8,128,128]{3,2,1,0:T(8,128)} %get-tuple-element.12.local, s16[8,256,128]{2,1,0:T(8,128)(2,1)} %get-tuple-element.13.side, s16[8,128,256]{2,1,0:T(8,128)(2,1)} %get-tuple-element.14.back), custom_call_target="tpu_custom_call" | custom-call | tf_op jit(solution)/shard_map/pallas_call | solution.py:552

commit v3 on v2

--- a/solution.py
+++ b/solution.py
@@ -200,7 +200,8 @@
      sums_out, sums_core, sums_chip, sums_x, scale_own, scale_side, scale_first, scale_second,
      columns, pair_columns, lanes,
      core_send, core_recv, x_send, x_recv, up_send, up_recv, back_send, back_recv,
-     side_send, side_recv, diag_send, diag_recv, pair_send, pair_recv, sum_send, sum_recv, keep_sem) = refs
+     side_send, side_recv, diag_send, diag_recv, pair_send, pair_recv, sum_send, sum_recv, keep_sem,
+     y_send, y_recv, diag_core_send, diag_core_recv, pair_core_send, pair_core_recv) = refs
     frames, pixels = counts.shape
     step, last = frames // CHUNKS, 2 * CHUNKS - 1
     at_tm, at_pix = lax.axis_index("tm"), lax.axis_index("pix")
@@ -244,7 +245,15 @@
     def chunk(n):
         return pl.ds(pl.multiple_of(n * step, step), step)
 
-    by_side = start(right.at[own], right.at[beside], side_send.at[0], side_recv.at[0], to_y)
+    deep = pixels // 2
+
+    def depth(h):
+        return pl.ds(h * deep, deep)
+
+    by_side = [
+        start(right.at[own, depth(h)], right.at[beside, depth(h)], y_send.at[h], y_recv.at[h], to_y)
+        for h in range(2)
+    ]
 
     def to_ring(n):
         return remote(right.at[chunk(n)], ring.at[chunk(n)], up_send.at[n], up_recv.at[n], to_up)
@@ -285,36 +294,50 @@
     for n in range(1, CHUNKS):
         to_ring(n).start()
 
-    away_base, own_base = (1 - x) * 2 * owned, x * 2 * owned
-
-    def reduce_unit(left, rows, count, cols, made, to_other, inn, code_out, to_across, kept):
-        def product(j, carry):
-            owner_core = lax.rem(core + 1 + j, 2)
-            block = left[rows, :].reshape(count // TILE, TILE, pixels)
-            masked = jnp.concatenate(
-                [
-                    (block * wide[base + owner_core * owned + i][None]).reshape(count, pixels)
-                    for base in (away_base, own_base)
-                    for i in range(owned)
-                ],
-                axis=0,
-            )
-            value = lax.dot_general(
-                masked, right[cols, :], (((1,), (1,)), ((), ())), preferred_element_type=jnp.float32
-            )
-            made[j] = value.reshape(2, owned, count, cols.size)
+    def product(left, rows, count, cols, made, j, ks, add):
+        base = (lax.rem(x + 1 + j, 2) * 2 + lax.rem(core + 1 + j // 2, 2)) * owned
+        block = left[rows, ks].reshape(count // TILE, TILE, ks.size)
+        masked = jnp.concatenate(
+            [(block * wide[base + i, :, ks][None]).reshape(count, ks.size) for i in range(owned)],
+            axis=0,
+        )
+        value = lax.dot_general(
+            masked, right[cols, ks], (((1,), (1,)), ((), ())), preferred_element_type=jnp.float32
+        ).reshape(owned, count, cols.size)
+        made[j] = made[j] + value if add else value
+
+    def early(left, rows, count, cols, made):
+        def body(j, carry):
+            product(left, rows, count, cols, made, j, depth(0), False)
+            return carry
+
+        lax.fori_loop(0, 4, body, 0)
+
+    def reduce_unit(left, rows, count, cols, made, others, inn, code_out, across, kept, late=False):
+        ks = depth(1) if late else pl.ds(0, pixels)
+
+        def body(j, carry):
+            product(left, rows, count, cols, made, j, ks, late)
 
             @pl.when(j == 0)
             def _():
-                to_other.start()
+                others[0].start()
+
+            @pl.when(j == 1)
+            def _():
+                others[1].start()
+
+            @pl.when(j == 2)
+            def _():
+                others[0].wait_recv()
+                code_out[...] = partials.encode(made[2] + inn[0])
+                across.start()
 
             return carry
 
-        lax.fori_loop(0, 2, product, 0)
-        to_other.wait_recv()
-        code_out[...] = partials.encode(made[1, 0] + inn[0])
-        to_across.start()
-        kept[...] = made[1, 1] + inn[1]
+        lax.fori_loop(0, 4, body, 0)
+        others[1].wait_recv()
+        kept[...] = made[3] + inn[1]
 
     half = frames // 2
 
@@ -322,11 +345,15 @@
         return pltpu.make_async_copy(source, target, keep_sem.at[n])
 
     def diag_core(n):
-        return remote(diag_out.at[n, 0], diag_in.at[n], diag_send.at[n], diag_recv.at[n], to_core)
+        return [
+            remote(diag_out.at[n, g], diag_in.at[n, g],
+                   diag_core_send.at[n, g], diag_core_recv.at[n, g], to_core)
+            for g in range(2)
+        ]
 
     def diag_across(n):
         return remote(diag_x_out.at[n], diag_x_in.at[n],
-                      diag_send.at[2 + n], diag_recv.at[2 + n], to_x)
+                      diag_send.at[n], diag_recv.at[n], to_x)
 
     def diag_unit(n, carry):
         rows = pl.ds(pl.multiple_of(n * half, half), half)
@@ -335,7 +362,7 @@
         return carry
 
     lax.fori_loop(0, 2, diag_unit, 0)
-    copies += [diag_core(0), diag_core(1), diag_across(0), diag_across(1)]
+    copies += [*diag_core(0), *diag_core(1), diag_across(0), diag_across(1)]
 
     def pass_on(n):
         remote(ring.at[chunk(n)], ring.at[chunk(n)], up_send.at[n], up_recv.at[n], to_up).wait_recv()
@@ -345,6 +372,16 @@
     by_up2 = start(scale_first, scale_second, sum_send.at[4], sum_recv.at[4], to_up)
     for n in range(CHUNKS - 1):
         pass_on(n)
+    half_rows = pl.ds(pl.multiple_of(y * half, half), half)
+    pair_block = (right, pl.ds(pl.multiple_of(y * (frames + half), half), half), half,
+                  pl.ds(pl.multiple_of((1 - y) * frames, frames), frames), pair_out)
+
+    def unit_block(n):
+        return ring, chunk(n), step, every, swap_out.at[n]
+
+    by_side[0].wait_recv()
+    early(*pair_block)
+    early(*unit_block(0))
     size = scale_own[:, beside]
     own_sums = scale_own[:, own]
     own_columns = jnp.transpose(size / own_sums, (1, 0))
@@ -358,15 +395,15 @@
             diag_rows[r, rows, :] = value * (1.0 / own_sums[r : r + 1])
     keep(diag_rows, diagonal, 0).start()
 
-    by_side.wait_recv()
+    pair_across = remote(pair_x_out, pair_x_in, pair_send.at[1], pair_recv.at[1], to_x)
+    pair_core = [
+        remote(pair_out.at[g], pair_in.at[g], pair_core_send.at[g], pair_core_recv.at[g], to_core)
+        for g in range(2)
+    ]
+    by_side[1].wait_recv()
     pass_on(CHUNKS - 1)
-    half_rows = pl.ds(pl.multiple_of(y * half, half), half)
-    pair_core = remote(pair_out.at[0], pair_in, pair_send.at[0], pair_recv.at[0], to_core)
-    pair_across = remote(pair_x_out, pair_x_in, pair_send.at[1], pair_recv.at[1], to_x)
-    reduce_unit(right, pl.ds(pl.multiple_of(y * (frames + half), half), half), half,
-                pl.ds(pl.multiple_of((1 - y) * frames, frames), frames),
-                pair_out, pair_core, pair_in, pair_x_out, pair_across, pair_here)
-    copies += [pair_core, pair_across]
+    reduce_unit(*pair_block, pair_core, pair_in, pair_x_out, pair_across, pair_here, late=True)
+    copies += [*pair_core, pair_across]
 
     by_y.wait_recv()
     side_sums = scale_side[:, own]
@@ -376,18 +413,22 @@
     lanes[...] = 1.0 / jnp.concatenate([own_sums, side_sums], axis=1)
 
     def to_other(n):
-        return remote(swap_out.at[n, 0], swap_in.at[n], core_send.at[n], core_recv.at[n], to_core)
+        return [
+            remote(swap_out.at[n, g], swap_in.at[n, g],
+                   core_send.at[n, g], core_recv.at[n, g], to_core)
+            for g in range(2)
+        ]
 
     def to_across(n):
         return remote(x_out.at[n], x_in.at[n], x_send.at[n], x_recv.at[n], to_x)
 
     def to_side(n):
-        return remote(side_out.at[n], side_in.at[:, chunk(n)], side_send.at[1 + n], side_recv.at[1 + n], to_y)
+        return remote(side_out.at[n], side_in.at[:, chunk(n)], side_send.at[n], side_recv.at[n], to_y)
 
     def to_back(n):
         return remote(back_out.at[n], back_in.at[:, chunk(n)], back_send.at[n], back_recv.at[n], to_down)
 
-    by_pair = remote(pair_rows, pair.at[:, half_rows], pair_send.at[2], pair_recv.at[2], to_y)
+    by_pair = remote(pair_rows, pair.at[:, half_rows], pair_send.at[0], pair_recv.at[0], to_y)
 
     def finish(n):
         to_across(n).wait_recv()
@@ -410,33 +451,24 @@
             local_turned[s, r] = jnp.transpose(local_rows[r, pl.ds(s * frames, frames), :], (1, 0))
         keep(local_turned.at[s], local.at[s], 1 + s).start()
 
+    def reduce_block(n, late=False):
+        reduce_unit(*unit_block(n), to_other(n), swap_in.at[n],
+                    x_out.at[n], to_across(n), here.at[n], late)
+
     def unit(n, carry):
         @pl.when(n >= CHUNKS)
         def _():
             remote(ring.at[chunk(n)], ring.at[chunk(n)],
                    up_send.at[n], up_recv.at[n], to_up).wait_recv()
 
-        reduce_unit(ring, chunk(n), step, every, swap_out.at[n], to_other(n), swap_in.at[n],
-                    x_out.at[n], to_across(n), here.at[n])
-
-        @pl.when(n == 0)
-        def _():
-            pair_across.wait_recv()
-            for r in range(owned):
-                value = pair_here[r] + partials.decode(pair_x_in[r])
-                value = value * pair_columns[half_rows, r : r + 1] * pair_lanes[r : r + 1]
-                pair_rows[r] = results.encode(value)
-            by_pair.start()
-            keep(pair_rows, pair.at[:, half_rows], 3).start()
-
-        @pl.when(n == 1)
+        reduce_block(n)
+
+        @pl.when(n == CHUNKS)
         def _():
             by_up2.wait_recv()
             columns[beside, :] = jnp.transpose(size / scale_second[:, own], (1, 0))
 
-        @pl.when(n > 0)
-        def _():
-            finish(n - 1)
+        finish(n - 1)
 
         @pl.when(n == CHUNKS)
         def _():
@@ -444,13 +476,21 @@
 
         return carry
 
-    lax.fori_loop(0, 2 * CHUNKS, unit, 0)
+    reduce_block(0, late=True)
+    pair_across.wait_recv()
+    for r in range(owned):
+        value = pair_here[r] + partials.decode(pair_x_in[r])
+        value = value * pair_columns[half_rows, r : r + 1] * pair_lanes[r : r + 1]
+        pair_rows[r] = results.encode(value)
+    by_pair.start()
+    keep(pair_rows, pair.at[:, half_rows], 3).start()
+    lax.fori_loop(1, 2 * CHUNKS, unit, 0)
     finish(jnp.int32(last))
     turn(1)
     by_pair.wait_recv()
     copies.append(by_pair)
     for n in range(2 * CHUNKS):
-        copies += [to_other(n), to_across(n), to_side(n)]
+        copies += [*to_other(n), to_across(n), to_side(n)]
         to_side(n).wait_recv()
     for n in range(CHUNKS):
         copies.append(to_back(n))
@@ -468,29 +508,24 @@
     at_tm = lax.axis_index("tm")
     z, y = at_tm // 2, at_tm % 2
 
-    def put(dz, dy, value):
-        block = (z + dz + 4) % 4 * 2 + (y + dy) % 2
-        out[0, :, pl.ds(pl.multiple_of(block * frames, frames), frames)] = value
-
     def turn(value):
         return jnp.transpose(value, (1, 0))
 
-    put(0, 0, diagonal[0])
-
-    @pl.when(y == 0)
-    def _():
-        put(0, 1, results.decode(pair[0]))
-
-    @pl.when(y == 1)
-    def _():
-        put(0, 1, turn(results.decode(pair[0])))
-
-    for s in range(2):
-        put(-1 - s, 0, local[s, 0])
-        put(-1 - s, 1, turn(results.decode(side[0, pl.ds(s * frames, frames), :])))
-    value = results.decode(back[0])
-    put(1, 0, value[:, :frames])
-    put(1, 1, value[:, frames:])
+    for r in range(diagonal.shape[0]):
+
+        def put(dz, dy, value):
+            block = (z + dz + 4) % 4 * 2 + (y + dy) % 2
+            out[r, :, pl.ds(pl.multiple_of(block * frames, frames), frames)] = value
+
+        put(0, 0, diagonal[r])
+        value = results.decode(pair[r])
+        put(0, 1, jnp.where(y == 0, value, turn(value)))
+        for s in range(2):
+            put(-1 - s, 0, local[s, r])
+            put(-1 - s, 1, turn(results.decode(side[r, pl.ds(s * frames, frames), :])))
+        value = results.decode(back[r])
+        put(1, 0, value[:, :frames])
+        put(1, 1, value[:, frames:])
 
 
 def per_device_kernel(counts, dead_time, flat_field, cycle_map):
@@ -511,17 +546,17 @@
         vmem((CYCLES, TILE, pixels), bf16),
         vmem((both, pixels), bf16),
         vmem((both, pixels), bf16),
-        vmem((units, 2, 2, owned, step, both), f32),
+        vmem((units, 4, owned, step, both), f32),
         vmem((units, 2, owned, step, both), f32),
         *[vmem((units, owned, step, both), i16)] * 2,
         vmem((units, owned, step, both), f32),
         vmem((units, owned, step, frames), i16),
         vmem((units, owned, step, both), i16),
-        vmem((2, 2, 2, owned, half, frames), f32),
+        vmem((2, 4, owned, half, frames), f32),
         vmem((2, 2, owned, half, frames), f32),
         *[vmem((2, owned, half, frames), i16)] * 2,
         vmem((2, owned, half, frames), f32),
-        vmem((2, 2, owned, half, frames), f32),
+        vmem((4, owned, half, frames), f32),
         vmem((2, owned, half, frames), f32),
         *[vmem((owned, half, frames), i16)] * 2,
         vmem((owned, half, frames), f32),
@@ -530,10 +565,10 @@
         vmem((both, owned), f32),
         vmem((frames, owned), f32),
         vmem(small, f32),
-        dma((units,)), dma((units,)), dma((units,)), dma((units,)),
+        dma((units, 2)), dma((units, 2)), dma((units,)), dma((units,)),
         dma((units,)), dma((units,)), dma((CHUNKS,)), dma((CHUNKS,)),
-        dma((1 + units,)), dma((1 + units,)), dma((4,)), dma((4,)), dma((3,)), dma((3,)),
-        dma((5,)), dma((5,)), dma((4,)),
+        dma((units,)), dma((units,)), dma((2,)), dma((2,)), dma((2,)), dma((2,)),
+        dma((5,)), dma((5,)), dma((4,)), dma((2,)), dma((2,)), dma((2, 2)), dma((2, 2)), dma((2,)), dma((2,)),
     ]
     shapes = [
         ((owned, frames, frames), f32), ((owned, frames, frames), i16),
@@ -549,17 +584,18 @@
             collective_id=0, has_side_effects=True, vmem_limit_bytes=60 << 20
         ),
     )(counts, dead_time[None, :], flat_field[None, :], cycle_map[None, :])
+    group = owned // 2
     return pl.pallas_call(
         functools.partial(assemble, results),
-        grid=(owned,),
+        grid=(owned // group,),
         out_shape=jax.ShapeDtypeStruct((owned, frames, tm * frames), f32),
         in_specs=[
-            pl.BlockSpec((1, *shape[1:]), lambda r: (r, 0, 0))
+            pl.BlockSpec((group, *shape[1:]), lambda r: (r, 0, 0))
             if len(shape) == 3
-            else pl.BlockSpec((shape[0], 1, *shape[2:]), lambda r: (0, r, 0, 0))
+            else pl.BlockSpec((shape[0], group, *shape[2:]), lambda r: (0, r, 0, 0))
             for shape, _ in shapes
         ],
-        out_specs=pl.BlockSpec((1, frames, tm * frames), lambda r: (r, 0, 0)),
+        out_specs=pl.BlockSpec((group, frames, tm * frames), lambda r: (r, 0, 0)),
     )(*pieces)
 
 

time: 82 us -> 75.1 us (0.916)
  Pallas kernels: 81.7 us -> 74.9 us
    pallas_call x1, Pallas kernels: 74.9 us -> 71.1 us  [per_device_kernel(): pl.pallas_call(functools.partial(exchange, owned, partials, results), out...]
    pallas_call x1, Pallas kernels: 6.81 us -> 3.78 us  [per_device_kernel(): pl.pallas_call(functools.partial(assemble, results), grid=(owned // group...]
where the time goes in v3:
time: 75.1 us; the launch traced here: 74.9 us
  Pallas kernels  74.9 us (100%)
    pallas_call x1, Pallas kernels, per_device_kernel(): pl.pallas_call(functools.partial(exchange, owned, partials, results), out...  71.1 us
    pallas_call x1, Pallas kernels, per_device_kernel(): pl.pallas_call(functools.partial(assemble, results), grid=(owned // group...  3.78 us

profile of v3, /device:TPU:0, one launch (start us, length us, event | category | flops | bytes accessed | tf_op | source)
XLA Modules:
  0.0 74.9 jit_solution(456465165257223083)
XLA Ops:
  0.0 71.1 %shard_map.46 = (f32[8,128,128]{2,1,0:T(8,128)}, s16[8,128,128]{2,1,0:T(8,128)(2,1)}, f32[2,8,128,128]{3,2,1,0:T(8,128)}, s16[8,256,128]{2,1,0:T(8,128)(2,1)}, s16[8,128,256]{2,1,0:T(8,128)(2,1)}) custom-call(f32[128,4096]{1,0:T(8,128)} %refs_0_.1, f32[1,4096]{1,0:T(1,128)} %bitcast.3, f32[1,4096]{1,0:T(1,128)} %bitcast.4, s32[1,4096]{1,0:T(1,128)} %bitcast.5), custom_call_target="tpu_custom_call" | custom-call | tf_op jit(solution)/shard_map/pallas_call | solution.py:577
  71.1 3.8 %shard_map.47 = f32[8,128,1024]{2,1,0:T(8,128)} custom-call(f32[8,128,128]{2,1,0:T(8,128)} %get-tuple-element.10.diagonal, s16[8,128,128]{2,1,0:T(8,128)(2,1)} %get-tuple-element.11.pair, f32[2,8,128,128]{3,2,1,0:T(8,128)} %get-tuple-element.12.local, s16[8,256,128]{2,1,0:T(8,128)(2,1)} %get-tuple-element.13.side, s16[8,128,256]{2,1,0:T(8,128)(2,1)} %get-tuple-element.14.back), custom_call_target="tpu_custom_call" | custom-call | tf_op jit(solution)/shard_map/pallas_call | solution.py:588

commit v4 on v3

--- a/solution.py
+++ b/solution.py
@@ -184,6 +184,7 @@
 MESH = pl.DeviceIdType.MESH
 TILE = 16
 CHUNKS = 2
+PIECES = 4
 
 
 def fits_kernel(shape):
@@ -201,9 +202,12 @@
      columns, pair_columns, lanes,
      core_send, core_recv, x_send, x_recv, up_send, up_recv, back_send, back_recv,
      side_send, side_recv, diag_send, diag_recv, pair_send, pair_recv, sum_send, sum_recv, keep_sem,
-     y_send, y_recv, diag_core_send, diag_core_recv, pair_core_send, pair_core_recv) = refs
+     y_send, y_recv, diag_core_send, diag_core_recv, pair_core_send, pair_core_recv,
+     fine_swap_out, fine_swap_in, fine_x_out, fine_x_in, fine_here, fine_side_out,
+     fine_core_send, fine_core_recv, fine_x_send, fine_x_recv, fine_side_send, fine_side_recv,
+     raw_counts, load_sem) = refs
     frames, pixels = counts.shape
-    step, last = frames // CHUNKS, 2 * CHUNKS - 1
+    step, fine = frames // CHUNKS, frames // PIECES
     at_tm, at_pix = lax.axis_index("tm"), lax.axis_index("pix")
     z, y = at_tm // 2, at_tm % 2
     x, core = at_pix // 2, at_pix % 2
@@ -218,15 +222,23 @@
     for target in (to_y, to_up, to_down, to_core, to_x):
         pl.semaphore_signal(barrier, inc=1, device_id=target, device_id_type=MESH)
 
+    loads = [
+        pltpu.make_async_copy(counts.at[rows], raw_counts.at[rows], load_sem.at[q])
+        for q, rows in enumerate(pl.ds(q * fine, fine) for q in range(PIECES))
+    ]
+    for load in loads:
+        load.start()
+
     def correct(i, carry):
         rows = pl.ds(pl.multiple_of(i * TILE, TILE), TILE)
-        raw = counts[rows, :]
+        raw = raw_counts[rows, :]
         value = raw / (1.0 - dead_time[...] * raw) * flat_field[...]
         right[rows, :] = value.astype(jnp.bfloat16)
         return carry
 
-    lax.fori_loop(0, frames // TILE, correct, 0)
-    pl.semaphore_wait(barrier, 5)
+    def correct_piece(q):
+        loads[q].wait()
+        lax.fori_loop(q * fine // TILE, (q + 1) * fine // TILE, correct, 0)
 
     def remote(source, target, send, recv, device):
         return pltpu.make_async_remote_copy(
@@ -245,6 +257,17 @@
     def chunk(n):
         return pl.ds(pl.multiple_of(n * step, step), step)
 
+    for q in range(PIECES // CHUNKS):
+        correct_piece(q)
+    pl.semaphore_wait(barrier, 5)
+
+    def to_ring(n):
+        return remote(right.at[chunk(n)], ring.at[chunk(n)], up_send.at[n], up_recv.at[n], to_up)
+
+    to_rings = [to_ring(n) for n in range(CHUNKS)]
+    to_rings[0].start()
+    for q in range(PIECES // CHUNKS, PIECES):
+        correct_piece(q)
     deep = pixels // 2
 
     def depth(h):
@@ -255,15 +278,15 @@
         for h in range(2)
     ]
 
-    def to_ring(n):
-        return remote(right.at[chunk(n)], ring.at[chunk(n)], up_send.at[n], up_recv.at[n], to_up)
-
-    def forward(n):
-        return remote(ring.at[chunk(n)], ring.at[chunk(n + CHUNKS)],
-                      up_send.at[n + CHUNKS], up_recv.at[n + CHUNKS], to_up)
-
-    copies += [to_ring(n) for n in range(CHUNKS)] + [forward(n) for n in range(CHUNKS)]
-    to_ring(0).start()
+    def piece(m, offset=0):
+        return pl.ds(pl.multiple_of(offset + m * fine, fine), fine)
+
+    def forward(m):
+        return remote(ring.at[piece(m)], ring.at[piece(m, frames)],
+                      up_send.at[m + CHUNKS], up_recv.at[m + CHUNKS], to_up)
+
+    landed = [forward(m) for m in range(PIECES)]
+    copies += to_rings + landed
 
     ids = lax.broadcasted_iota(jnp.int32, (CYCLES, pixels), 0)
     onehot = jnp.where(jnp.broadcast_to(cycle_map[...], (CYCLES, pixels)) == ids, 1.0, 0.0)
@@ -292,7 +315,7 @@
     by_y = start(scale_own, scale_side, sum_send.at[2], sum_recv.at[2], to_y)
     by_up = start(scale_own, scale_first, sum_send.at[3], sum_recv.at[3], to_up)
     for n in range(1, CHUNKS):
-        to_ring(n).start()
+        to_rings[n].start()
 
     def product(left, rows, count, cols, made, j, ks, add):
         base = (lax.rem(x + 1 + j, 2) * 2 + lax.rem(core + 1 + j // 2, 2)) * owned
@@ -313,31 +336,36 @@
 
         lax.fori_loop(0, 4, body, 0)
 
-    def reduce_unit(left, rows, count, cols, made, others, inn, code_out, across, kept, late=False):
+    def send_across(unit):
+        unit["others"][0].wait_recv()
+        unit["code_out"][...] = partials.encode(unit["block"][4][2] + unit["inn"][0])
+        unit["across"].start()
+
+    def settle(unit):
+        unit["others"][1].wait_recv()
+        unit["here"][...] = unit["block"][4][3] + unit["inn"][1]
+
+    def reduce_unit(unit, before=None, late=False):
         ks = depth(1) if late else pl.ds(0, pixels)
 
         def body(j, carry):
-            product(left, rows, count, cols, made, j, ks, late)
+            product(*unit["block"], j, ks, late)
 
             @pl.when(j == 0)
             def _():
-                others[0].start()
+                unit["others"][0].start()
+                if before is not None:
+                    send_across(before)
 
             @pl.when(j == 1)
             def _():
-                others[1].start()
-
-            @pl.when(j == 2)
-            def _():
-                others[0].wait_recv()
-                code_out[...] = partials.encode(made[2] + inn[0])
-                across.start()
+                unit["others"][1].start()
+                if before is not None:
+                    settle(before)
 
             return carry
 
         lax.fori_loop(0, 4, body, 0)
-        others[1].wait_recv()
-        kept[...] = made[3] + inn[1]
 
     half = frames // 2
 
@@ -355,18 +383,22 @@
         return remote(diag_x_out.at[n], diag_x_in.at[n],
                       diag_send.at[n], diag_recv.at[n], to_x)
 
-    def diag_unit(n, carry):
-        rows = pl.ds(pl.multiple_of(n * half, half), half)
-        reduce_unit(right, rows, half, own, diag_out.at[n], diag_core(n), diag_in.at[n],
-                    diag_x_out.at[n], diag_across(n), diag_here.at[n])
-        return carry
-
-    lax.fori_loop(0, 2, diag_unit, 0)
-    copies += [*diag_core(0), *diag_core(1), diag_across(0), diag_across(1)]
+    def diag_unit(n):
+        return dict(
+            block=(right, pl.ds(n * half, half), half, own, diag_out.at[n]), inn=diag_in.at[n],
+            others=diag_core(n), code_out=diag_x_out.at[n], across=diag_across(n), here=diag_here.at[n],
+        )
+
+    diags = [diag_unit(0), diag_unit(1)]
+    reduce_unit(diags[0])
+    reduce_unit(diags[1], diags[0])
+    for unit in diags:
+        copies += [*unit["others"], unit["across"]]
 
     def pass_on(n):
         remote(ring.at[chunk(n)], ring.at[chunk(n)], up_send.at[n], up_recv.at[n], to_up).wait_recv()
-        forward(n).start()
+        for m in range(n * PIECES // CHUNKS, (n + 1) * PIECES // CHUNKS):
+            landed[m].start()
 
     by_up.wait_recv()
     by_up2 = start(scale_first, scale_second, sum_send.at[4], sum_recv.at[4], to_up)
@@ -376,19 +408,18 @@
     pair_block = (right, pl.ds(pl.multiple_of(y * (frames + half), half), half), half,
                   pl.ds(pl.multiple_of((1 - y) * frames, frames), frames), pair_out)
 
-    def unit_block(n):
-        return ring, chunk(n), step, every, swap_out.at[n]
-
     by_side[0].wait_recv()
     early(*pair_block)
-    early(*unit_block(0))
+    send_across(diags[1])
+    settle(diags[1])
+    early(ring, chunk(0), step, every, swap_out.at[0])
     size = scale_own[:, beside]
     own_sums = scale_own[:, own]
     own_columns = jnp.transpose(size / own_sums, (1, 0))
     columns[own, :] = jnp.transpose(size / scale_first[:, own], (1, 0))
     for n in range(2):
         rows = pl.ds(n * half, half)
-        diag_across(n).wait_recv()
+        diags[n]["across"].wait_recv()
         for r in range(owned):
             value = diag_here[n, r] + partials.decode(diag_x_in[n, r])
             value = value * own_columns[n * half : (n + 1) * half, r : r + 1]
@@ -402,7 +433,9 @@
     ]
     by_side[1].wait_recv()
     pass_on(CHUNKS - 1)
-    reduce_unit(*pair_block, pair_core, pair_in, pair_x_out, pair_across, pair_here, late=True)
+    pair_unit = dict(block=pair_block, others=pair_core, inn=pair_in, code_out=pair_x_out,
+                     across=pair_across, here=pair_here)
+    reduce_unit(pair_unit, late=True)
     copies += [*pair_core, pair_across]
 
     by_y.wait_recv()
@@ -412,89 +445,87 @@
     pair_lanes = 1.0 / jnp.where(lower, side_sums, own_sums)
     lanes[...] = 1.0 / jnp.concatenate([own_sums, side_sums], axis=1)
 
-    def to_other(n):
-        return [
-            remote(swap_out.at[n, g], swap_in.at[n, g],
-                   core_send.at[n, g], core_recv.at[n, g], to_core)
-            for g in range(2)
-        ]
-
-    def to_across(n):
-        return remote(x_out.at[n], x_in.at[n], x_send.at[n], x_recv.at[n], to_x)
-
-    def to_side(n):
-        return remote(side_out.at[n], side_in.at[:, chunk(n)], side_send.at[n], side_recv.at[n], to_y)
-
-    def to_back(n):
-        return remote(back_out.at[n], back_in.at[:, chunk(n)], back_send.at[n], back_recv.at[n], to_down)
+    def coarse(n):
+        rows = chunk(n)
+        return dict(
+            block=(ring, rows, step, every, swap_out.at[n]), rows=rows, inn=swap_in.at[n],
+            others=[remote(swap_out.at[n, g], swap_in.at[n, g],
+                           core_send.at[n, g], core_recv.at[n, g], to_core) for g in range(2)],
+            code_out=x_out.at[n], code_in=x_in.at[n],
+            across=remote(x_out.at[n], x_in.at[n], x_send.at[n], x_recv.at[n], to_x),
+            here=here.at[n], side=side_out.at[n], back=back_out.at[n],
+            to_side=remote(side_out.at[n], side_in.at[:, rows], side_send.at[n], side_recv.at[n], to_y),
+            to_back=remote(back_out.at[n], back_in.at[:, rows], back_send.at[n], back_recv.at[n], to_down),
+        )
+
+    def fine_unit(m):
+        rows = piece(m, frames)
+        return dict(
+            block=(ring, rows, fine, every, fine_swap_out.at[m]), rows=rows, inn=fine_swap_in.at[m],
+            others=[remote(fine_swap_out.at[m, g], fine_swap_in.at[m, g],
+                           fine_core_send.at[m, g], fine_core_recv.at[m, g], to_core)
+                    for g in range(2)],
+            code_out=fine_x_out.at[m], code_in=fine_x_in.at[m],
+            across=remote(fine_x_out.at[m], fine_x_in.at[m], fine_x_send.at[m], fine_x_recv.at[m], to_x),
+            here=fine_here.at[m], side=fine_side_out.at[m], back=None,
+            to_side=remote(fine_side_out.at[m], side_in.at[:, rows],
+                           fine_side_send.at[m], fine_side_recv.at[m], to_y),
+        )
 
     by_pair = remote(pair_rows, pair.at[:, half_rows], pair_send.at[0], pair_recv.at[0], to_y)
 
-    def finish(n):
-        to_across(n).wait_recv()
-
+    def finish(unit):
+        unit["across"].wait_recv()
+        rows, back = unit["rows"], unit["back"]
         for r in range(owned):
-            value = here[n, r] + partials.decode(x_in[n, r])
-            value = value * columns[chunk(n), r : r + 1] * lanes[r : r + 1, :]
-            back_out[n, r] = results.encode(value)
-            side_out[n, r] = results.encode(value[:, frames:])
-            local_rows[r, chunk(n), :] = value[:, :frames]
-
-        @pl.when(n < CHUNKS)
-        def _():
-            to_back(n).start()
-
-        to_side(n).start()
+            value = unit["here"][r] + partials.decode(unit["code_in"][r])
+            value = value * columns[rows, r : r + 1] * lanes[r : r + 1, :]
+            if back is not None:
+                back[r] = results.encode(value)
+            unit["side"][r] = results.encode(value[:, frames:])
+            local_rows[r, rows, :] = value[:, :frames]
+        if back is not None:
+            unit["to_back"].start()
+        unit["to_side"].start()
 
     def turn(s):
         for r in range(owned):
             local_turned[s, r] = jnp.transpose(local_rows[r, pl.ds(s * frames, frames), :], (1, 0))
         keep(local_turned.at[s], local.at[s], 1 + s).start()
 
-    def reduce_block(n, late=False):
-        reduce_unit(*unit_block(n), to_other(n), swap_in.at[n],
-                    x_out.at[n], to_across(n), here.at[n], late)
-
-    def unit(n, carry):
-        @pl.when(n >= CHUNKS)
-        def _():
-            remote(ring.at[chunk(n)], ring.at[chunk(n)],
-                   up_send.at[n], up_recv.at[n], to_up).wait_recv()
-
-        reduce_block(n)
-
-        @pl.when(n == CHUNKS)
-        def _():
+    chain = [*map(coarse, range(CHUNKS)), *map(fine_unit, range(PIECES))]
+    for k, unit in enumerate(chain):
+        if k >= CHUNKS:
+            landed[k - CHUNKS].wait_recv()
+        reduce_unit(unit, chain[k - 1] if k else pair_unit, late=k == 0)
+        if k == len(chain) - 1:
+            send_across(unit)
+        if k == 1:
+            pair_across.wait_recv()
+            for r in range(owned):
+                value = pair_here[r] + partials.decode(pair_x_in[r])
+                value = value * pair_columns[half_rows, r : r + 1] * pair_lanes[r : r + 1]
+                pair_rows[r] = results.encode(value)
+            by_pair.start()
+            keep(pair_rows, pair.at[:, half_rows], 3).start()
+        if k >= 2:
+            finish(chain[k - 2])
+        if k == CHUNKS:
             by_up2.wait_recv()
             columns[beside, :] = jnp.transpose(size / scale_second[:, own], (1, 0))
-
-        finish(n - 1)
-
-        @pl.when(n == CHUNKS)
-        def _():
+        if k == CHUNKS + 1:
             turn(0)
-
-        return carry
-
-    reduce_block(0, late=True)
-    pair_across.wait_recv()
-    for r in range(owned):
-        value = pair_here[r] + partials.decode(pair_x_in[r])
-        value = value * pair_columns[half_rows, r : r + 1] * pair_lanes[r : r + 1]
-        pair_rows[r] = results.encode(value)
-    by_pair.start()
-    keep(pair_rows, pair.at[:, half_rows], 3).start()
-    lax.fori_loop(1, 2 * CHUNKS, unit, 0)
-    finish(jnp.int32(last))
+    settle(chain[-1])
+    finish(chain[-2])
+    finish(chain[-1])
     turn(1)
     by_pair.wait_recv()
     copies.append(by_pair)
-    for n in range(2 * CHUNKS):
-        copies += [*to_other(n), to_across(n), to_side(n)]
-        to_side(n).wait_recv()
-    for n in range(CHUNKS):
-        copies.append(to_back(n))
-        to_back(n).wait_recv()
+    for unit in chain:
+        landing = [unit["to_side"]] + ([] if unit["back"] is None else [unit["to_back"]])
+        for copy in landing:
+            copy.wait_recv()
+        copies += [*unit["others"], unit["across"], *landing]
     keep(diag_rows, diagonal, 0).wait()
     for s in range(2):
         keep(local_turned.at[s], local.at[s], 1 + s).wait()
@@ -530,13 +561,16 @@
 
 def per_device_kernel(counts, dead_time, flat_field, cycle_map):
     frames, pixels = counts.shape
+    if frames % (PIECES * TILE):
+        return per_device(counts, dead_time, flat_field, cycle_map)
     tm, pix = lax.axis_size("tm"), lax.axis_size("pix")
     owned = CYCLES // pix
     partials = LogCode(0.0218, 6800.0 * pixels * 2, True)
     results = LogCode(1 / 140.0, 140.0, False)
     f32, bf16, i16 = jnp.float32, jnp.bfloat16, jnp.int16
     vmem, dma = pltpu.VMEM, pltpu.SemaphoreType.DMA
-    both, half, step, units = 2 * frames, frames // 2, frames // CHUNKS, 2 * CHUNKS
+    both, half, step, fine = 2 * frames, frames // 2, frames // CHUNKS, frames // PIECES
+    units, pieces, rings = CHUNKS, PIECES, CHUNKS + PIECES
     small = (owned, both)
     scratch = [
         vmem((owned, frames, frames), f32),
@@ -566,18 +600,25 @@
         vmem((frames, owned), f32),
         vmem(small, f32),
         dma((units, 2)), dma((units, 2)), dma((units,)), dma((units,)),
-        dma((units,)), dma((units,)), dma((CHUNKS,)), dma((CHUNKS,)),
+        dma((rings,)), dma((rings,)), dma((CHUNKS,)), dma((CHUNKS,)),
         dma((units,)), dma((units,)), dma((2,)), dma((2,)), dma((2,)), dma((2,)),
         dma((5,)), dma((5,)), dma((4,)), dma((2,)), dma((2,)), dma((2, 2)), dma((2, 2)), dma((2,)), dma((2,)),
+        vmem((pieces, 4, owned, fine, both), f32),
+        vmem((pieces, 2, owned, fine, both), f32),
+        *[vmem((pieces, owned, fine, both), i16)] * 2,
+        vmem((pieces, owned, fine, both), f32),
+        vmem((pieces, owned, fine, frames), i16),
+        dma((pieces, 2)), dma((pieces, 2)), dma((pieces,)), dma((pieces,)), dma((pieces,)), dma((pieces,)),
+        vmem((frames, pixels), f32), dma((pieces,)),
     ]
     shapes = [
         ((owned, frames, frames), f32), ((owned, frames, frames), i16),
         ((2, owned, frames, frames), f32), ((owned, both, frames), i16), ((owned, frames, both), i16),
     ]
-    pieces = pl.pallas_call(
+    made = pl.pallas_call(
         functools.partial(exchange, owned, partials, results),
         out_shape=[jax.ShapeDtypeStruct(*shape) for shape in shapes],
-        in_specs=[pl.BlockSpec(memory_space=pltpu.VMEM)] * 4,
+        in_specs=[pl.BlockSpec(memory_space=pl.ANY)] + [pl.BlockSpec(memory_space=pltpu.VMEM)] * 3,
         out_specs=[pl.BlockSpec(memory_space=pl.ANY)] * 5,
         scratch_shapes=scratch,
         compiler_params=pltpu.CompilerParams(
@@ -596,7 +637,7 @@
             for shape, _ in shapes
         ],
         out_specs=pl.BlockSpec((group, frames, tm * frames), lambda r: (r, 0, 0)),
-    )(*pieces)
+    )(*made)
 
 
 def solution(mesh):

time: 75.1 us -> 72.6 us (0.967)
  Pallas kernels: 74.9 us -> 72.2 us
    pallas_call x1, Pallas kernels: 71.1 us -> 68.5 us  [per_device_kernel(): pl.pallas_call(functools.partial(exchange, owned, partials, results), out...]
where the time goes in v4:
time: 72.6 us; the launch traced here: 72.3 us
  Pallas kernels  72.2 us (99%)
    pallas_call x1, Pallas kernels, per_device_kernel(): pl.pallas_call(functools.partial(exchange, owned, partials, results), out...  68.5 us
    pallas_call x1, Pallas kernels, per_device_kernel(): pl.pallas_call(functools.partial(assemble, results), grid=(owned // group...  3.78 us

profile of v4, /device:TPU:0, one launch (start us, length us, event | category | flops | bytes accessed | tf_op | source)
XLA Modules:
  0.0 72.3 jit_solution(17879771140179400416)
XLA Ops:
  0.0 68.5 %shard_map.46 = (f32[8,128,128]{2,1,0:T(8,128)}, s16[8,128,128]{2,1,0:T(8,128)(2,1)}, f32[2,8,128,128]{3,2,1,0:T(8,128)}, s16[8,256,128]{2,1,0:T(8,128)(2,1)}, s16[8,128,256]{2,1,0:T(8,128)(2,1)}) custom-call(f32[128,4096]{1,0:T(8,128)} %refs_0_.1, f32[1,4096]{1,0:T(1,128)} %bitcast.3, f32[1,4096]{1,0:T(1,128)} %bitcast.4, s32[1,4096]{1,0:T(1,128)} %bitcast.5), custom_call_target="tpu_custom_call" | custom-call | tf_op jit(solution)/shard_map/pallas_call | solution.py:618
  68.5 3.8 %shard_map.47 = f32[8,128,1024]{2,1,0:T(8,128)} custom-call(f32[8,128,128]{2,1,0:T(8,128)} %get-tuple-element.10.diagonal, s16[8,128,128]{2,1,0:T(8,128)(2,1)} %get-tuple-element.11.pair, f32[2,8,128,128]{3,2,1,0:T(8,128)} %get-tuple-element.12.local, s16[8,256,128]{2,1,0:T(8,128)(2,1)} %get-tuple-element.13.side, s16[8,128,256]{2,1,0:T(8,128)(2,1)} %get-tuple-element.14.back), custom_call_target="tpu_custom_call" | custom-call | tf_op jit(solution)/shard_map/pallas_call | solution.py:629

commit v5 on v4

--- a/solution.py
+++ b/solution.py
@@ -185,6 +185,8 @@
 TILE = 16
 CHUNKS = 2
 PIECES = 4
+LAG = 3
+GROUP = 2
 
 
 def fits_kernel(shape):
@@ -193,7 +195,7 @@
 
 
 def exchange(owned, partials, results, *refs):
-    (counts, dead_time, flat_field, cycle_map,
+    (counts, dead_source, flat_source, cycle_source,
      diagonal, pair, local, side_in, back_in, diag_rows, pair_rows, local_rows, local_turned,
      wide, right, ring, swap_out, swap_in, x_out, x_in, here, side_out, back_out,
      diag_out, diag_in, diag_x_out, diag_x_in, diag_here,
@@ -205,7 +207,7 @@
      y_send, y_recv, diag_core_send, diag_core_recv, pair_core_send, pair_core_recv,
      fine_swap_out, fine_swap_in, fine_x_out, fine_x_in, fine_here, fine_side_out,
      fine_core_send, fine_core_recv, fine_x_send, fine_x_recv, fine_side_send, fine_side_recv,
-     raw_counts, load_sem) = refs
+     raw_counts, load_sem, dead_time, flat_field, cycle_map) = refs
     frames, pixels = counts.shape
     step, fine = frames // CHUNKS, frames // PIECES
     at_tm, at_pix = lax.axis_index("tm"), lax.axis_index("pix")
@@ -226,8 +228,16 @@
         pltpu.make_async_copy(counts.at[rows], raw_counts.at[rows], load_sem.at[q])
         for q, rows in enumerate(pl.ds(q * fine, fine) for q in range(PIECES))
     ]
-    for load in loads:
+    per_pixel = [
+        pltpu.make_async_copy(source, target, load_sem.at[PIECES + k])
+        for k, (source, target) in enumerate(
+            ((dead_source, dead_time), (flat_source, flat_field), (cycle_source, cycle_map))
+        )
+    ]
+    for load in [*per_pixel[:2], *loads, per_pixel[2]]:
         load.start()
+    for load in per_pixel[:2]:
+        load.wait()
 
     def correct(i, carry):
         rows = pl.ds(pl.multiple_of(i * TILE, TILE), TILE)
@@ -271,7 +281,7 @@
     deep = pixels // 2
 
     def depth(h):
-        return pl.ds(h * deep, deep)
+        return pl.ds(0, deep) if h == 0 else pl.ds(deep, pixels - deep)
 
     by_side = [
         start(right.at[own, depth(h)], right.at[beside, depth(h)], y_send.at[h], y_recv.at[h], to_y)
@@ -288,6 +298,7 @@
     landed = [forward(m) for m in range(PIECES)]
     copies += to_rings + landed
 
+    per_pixel[2].wait()
     ids = lax.broadcasted_iota(jnp.int32, (CYCLES, pixels), 0)
     onehot = jnp.where(jnp.broadcast_to(cycle_map[...], (CYCLES, pixels)) == ids, 1.0, 0.0)
     counted = lax.dot_general(
@@ -345,7 +356,7 @@
         unit["others"][1].wait_recv()
         unit["here"][...] = unit["block"][4][3] + unit["inn"][1]
 
-    def reduce_unit(unit, before=None, late=False):
+    def reduce_unit(unit, before=None, late=False, final=False):
         ks = depth(1) if late else pl.ds(0, pixels)
 
         def body(j, carry):
@@ -362,6 +373,12 @@
                 unit["others"][1].start()
                 if before is not None:
                     settle(before)
+
+            if final:
+
+                @pl.when(j == 2)
+                def _():
+                    send_across(unit)
 
             return carry
 
@@ -497,9 +514,7 @@
     for k, unit in enumerate(chain):
         if k >= CHUNKS:
             landed[k - CHUNKS].wait_recv()
-        reduce_unit(unit, chain[k - 1] if k else pair_unit, late=k == 0)
-        if k == len(chain) - 1:
-            send_across(unit)
+        reduce_unit(unit, chain[k - 1] if k else pair_unit, k == 0, k == len(chain) - 1)
         if k == 1:
             pair_across.wait_recv()
             for r in range(owned):
@@ -508,15 +523,16 @@
                 pair_rows[r] = results.encode(value)
             by_pair.start()
             keep(pair_rows, pair.at[:, half_rows], 3).start()
-        if k >= 2:
-            finish(chain[k - 2])
+        if k >= LAG:
+            finish(chain[k - LAG])
         if k == CHUNKS:
             by_up2.wait_recv()
             columns[beside, :] = jnp.transpose(size / scale_second[:, own], (1, 0))
-        if k == CHUNKS + 1:
+        if k == CHUNKS - 1 + LAG:
             turn(0)
     settle(chain[-1])
-    finish(chain[-2])
+    for unit in chain[-LAG:-1]:
+        finish(unit)
     finish(chain[-1])
     turn(1)
     by_pair.wait_recv()
@@ -534,7 +550,25 @@
         copy.wait_send()
 
 
-def assemble(results, diagonal, pair, local, side, back, out):
+def assemble(results, *refs):
+    inputs, out, held, rows, in_sem, out_sem = refs[:5], refs[5], refs[6:11], refs[11], refs[12], refs[13]
+    diagonal, pair, local, side, back = held
+    owned = diagonal.shape[0]
+
+    def cut(ref, r):
+        span = pl.ds(r, GROUP)
+        return ref.at[:, span] if len(ref.shape) == 4 else ref.at[span]
+
+    loads = [
+        [
+            pltpu.make_async_copy(cut(source, r), cut(target, r), in_sem.at[r // GROUP, k])
+            for k, (source, target) in enumerate(zip(inputs, held))
+        ]
+        for r in range(0, owned, GROUP)
+    ]
+    for group in loads:
+        for load in group:
+            load.start()
     frames = diagonal.shape[1]
     at_tm = lax.axis_index("tm")
     z, y = at_tm // 2, at_tm % 2
@@ -542,11 +576,15 @@
     def turn(value):
         return jnp.transpose(value, (1, 0))
 
-    for r in range(diagonal.shape[0]):
+    stores = []
+    for r in range(owned):
+        if r % GROUP == 0:
+            for load in loads[r // GROUP]:
+                load.wait()
 
         def put(dz, dy, value):
             block = (z + dz + 4) % 4 * 2 + (y + dy) % 2
-            out[r, :, pl.ds(pl.multiple_of(block * frames, frames), frames)] = value
+            rows[r, :, pl.ds(pl.multiple_of(block * frames, frames), frames)] = value
 
         put(0, 0, diagonal[r])
         value = results.decode(pair[r])
@@ -557,6 +595,12 @@
         value = results.decode(back[r])
         put(1, 0, value[:, :frames])
         put(1, 1, value[:, frames:])
+        if r % GROUP == GROUP - 1:
+            span = pl.ds(r - GROUP + 1, GROUP)
+            stores.append(pltpu.make_async_copy(rows.at[span], out.at[span], out_sem.at[r // GROUP]))
+            stores[-1].start()
+    for store in stores:
+        store.wait()
 
 
 def per_device_kernel(counts, dead_time, flat_field, cycle_map):
@@ -609,7 +653,8 @@
         vmem((pieces, owned, fine, both), f32),
         vmem((pieces, owned, fine, frames), i16),
         dma((pieces, 2)), dma((pieces, 2)), dma((pieces,)), dma((pieces,)), dma((pieces,)), dma((pieces,)),
-        vmem((frames, pixels), f32), dma((pieces,)),
+        vmem((frames, pixels), f32), dma((pieces + 3,)),
+        *[vmem((1, pixels), f32)] * 2, vmem((1, pixels), jnp.int32),
     ]
     shapes = [
         ((owned, frames, frames), f32), ((owned, frames, frames), i16),
@@ -618,25 +663,24 @@
     made = pl.pallas_call(
         functools.partial(exchange, owned, partials, results),
         out_shape=[jax.ShapeDtypeStruct(*shape) for shape in shapes],
-        in_specs=[pl.BlockSpec(memory_space=pl.ANY)] + [pl.BlockSpec(memory_space=pltpu.VMEM)] * 3,
+        in_specs=[pl.BlockSpec(memory_space=pl.ANY)] * 4,
         out_specs=[pl.BlockSpec(memory_space=pl.ANY)] * 5,
         scratch_shapes=scratch,
         compiler_params=pltpu.CompilerParams(
             collective_id=0, has_side_effects=True, vmem_limit_bytes=60 << 20
         ),
     )(counts, dead_time[None, :], flat_field[None, :], cycle_map[None, :])
-    group = owned // 2
     return pl.pallas_call(
         functools.partial(assemble, results),
-        grid=(owned // group,),
         out_shape=jax.ShapeDtypeStruct((owned, frames, tm * frames), f32),
-        in_specs=[
-            pl.BlockSpec((group, *shape[1:]), lambda r: (r, 0, 0))
-            if len(shape) == 3
-            else pl.BlockSpec((shape[0], group, *shape[2:]), lambda r: (0, r, 0, 0))
-            for shape, _ in shapes
+        in_specs=[pl.BlockSpec(memory_space=pl.ANY)] * len(shapes),
+        out_specs=pl.BlockSpec(memory_space=pl.ANY),
+        scratch_shapes=[
+            *[vmem(*shape) for shape in shapes],
+            vmem((owned, frames, tm * frames), f32),
+            dma((owned // GROUP, len(shapes))), dma((owned // GROUP,)),
         ],
-        out_specs=pl.BlockSpec((group, frames, tm * frames), lambda r: (r, 0, 0)),
+        compiler_params=pltpu.CompilerParams(vmem_limit_bytes=60 << 20),
     )(*made)
 
 

time: 72.6 us -> 70.4 us (0.970)
  Pallas kernels: 72.2 us -> 70.1 us
    pallas_call x1, Pallas kernels: 68.5 us -> 66.5 us  [per_device_kernel(): pl.pallas_call(functools.partial(exchange, owned, partials, results), out...]
where the time goes in v5:
time: 70.4 us; the launch traced here: 70.1 us
  Pallas kernels  70.1 us (100%)
    pallas_call x1, Pallas kernels, per_device_kernel(): pl.pallas_call(functools.partial(exchange, owned, partials, results), out...  66.5 us
    pallas_call x1, Pallas kernels, per_device_kernel(): pl.pallas_call(functools.partial(assemble, results), out_shape=jax.ShapeD...  3.6 us

profile of v5, /device:TPU:0, one launch (start us, length us, event | category | flops | bytes accessed | tf_op | source)
XLA Modules:
  0.0 70.1 jit_solution(1804124026405887070)
XLA Ops:
  0.0 66.5 %shard_map.46 = (f32[8,128,128]{2,1,0:T(8,128)}, s16[8,128,128]{2,1,0:T(8,128)(2,1)}, f32[2,8,128,128]{3,2,1,0:T(8,128)}, s16[8,256,128]{2,1,0:T(8,128)(2,1)}, s16[8,128,256]{2,1,0:T(8,128)(2,1)}) custom-call(f32[128,4096]{1,0:T(8,128)} %refs_0_.1, f32[1,4096]{1,0:T(1,128)} %bitcast.3, f32[1,4096]{1,0:T(1,128)} %bitcast.4, s32[1,4096]{1,0:T(1,128)} %bitcast.5), custom_call_target="tpu_custom_call" | custom-call | tf_op jit(solution)/shard_map/pallas_call | solution.py:663
  66.5 3.6 %shard_map.47 = f32[8,128,1024]{2,1,0:T(8,128)} custom-call(f32[8,128,128]{2,1,0:T(8,128)} %get-tuple-element.10.refs_0_, s16[8,128,128]{2,1,0:T(8,128)(2,1)} %get-tuple-element.11.refs_1_, f32[2,8,128,128]{3,2,1,0:T(8,128)} %get-tuple-element.12.refs_2_, s16[8,256,128]{2,1,0:T(8,128)(2,1)} %get-tuple-element.13.refs_3_, ...), custom_call_target="tpu_custom_call" | custom-call | tf_op jit(solution)/shard_map/pallas_call | solution.py:673

commit v6 on v5

--- a/solution.py
+++ b/solution.py
@@ -186,7 +186,7 @@
 CHUNKS = 2
 PIECES = 4
 LAG = 3
-GROUP = 2
+GROUP = 1
 
 
 def fits_kernel(shape):
@@ -214,8 +214,8 @@
     z, y = at_tm // 2, at_tm % 2
     x, core = at_pix // 2, at_pix % 2
     to_y = {"tm": z * 2 + 1 - y}
-    to_up = {"tm": (z + 1) % 4 * 2 + y}
-    to_down = {"tm": (z + 3) % 4 * 2 + y}
+    to_up = {"tm": (z + 3) % 4 * 2 + y}
+    to_down = {"tm": (z + 1) % 4 * 2 + y}
     to_core = {"pix": x * 2 + 1 - core}
     to_x = {"pix": (1 - x) * 2 + core}
     own, beside, every = pl.ds(0, frames), pl.ds(frames, frames), pl.ds(0, 2 * frames)
@@ -590,11 +590,11 @@
         value = results.decode(pair[r])
         put(0, 1, jnp.where(y == 0, value, turn(value)))
         for s in range(2):
-            put(-1 - s, 0, local[s, r])
-            put(-1 - s, 1, turn(results.decode(side[r, pl.ds(s * frames, frames), :])))
+            put(1 + s, 0, local[s, r])
+            put(1 + s, 1, turn(results.decode(side[r, pl.ds(s * frames, frames), :])))
         value = results.decode(back[r])
-        put(1, 0, value[:, :frames])
-        put(1, 1, value[:, frames:])
+        put(-1, 0, value[:, :frames])
+        put(-1, 1, value[:, frames:])
         if r % GROUP == GROUP - 1:
             span = pl.ds(r - GROUP + 1, GROUP)
             stores.append(pltpu.make_async_copy(rows.at[span], out.at[span], out_sem.at[r // GROUP]))

time: 70.4 us -> 68.9 us (0.979)
  Pallas kernels: 70.1 us -> 68.7 us
    pallas_call x1, Pallas kernels: 66.5 us -> 65.1 us  [per_device_kernel(): pl.pallas_call(functools.partial(exchange, owned, partials, results), out...]
where the time goes in v6:
time: 68.9 us; the launch traced here: 68.7 us
  Pallas kernels  68.7 us (100%)
    pallas_call x1, Pallas kernels, per_device_kernel(): pl.pallas_call(functools.partial(exchange, owned, partials, results), out...  65.1 us
    pallas_call x1, Pallas kernels, per_device_kernel(): pl.pallas_call(functools.partial(assemble, results), out_shape=jax.ShapeD...  3.59 us

profile of v6, /device:TPU:0, one launch (start us, length us, event | category | flops | bytes accessed | tf_op | source)
XLA Modules:
  0.0 68.7 jit_solution(8041651098600144461)
XLA Ops:
  0.0 65.1 %shard_map.46 = (f32[8,128,128]{2,1,0:T(8,128)}, s16[8,128,128]{2,1,0:T(8,128)(2,1)}, f32[2,8,128,128]{3,2,1,0:T(8,128)}, s16[8,256,128]{2,1,0:T(8,128)(2,1)}, s16[8,128,256]{2,1,0:T(8,128)(2,1)}) custom-call(f32[128,4096]{1,0:T(8,128)} %refs_0_.1, f32[1,4096]{1,0:T(1,128)} %bitcast.3, f32[1,4096]{1,0:T(1,128)} %bitcast.4, s32[1,4096]{1,0:T(1,128)} %bitcast.5), custom_call_target="tpu_custom_call" | custom-call | tf_op jit(solution)/shard_map/pallas_call | solution.py:663
  65.1 3.6 %shard_map.47 = f32[8,128,1024]{2,1,0:T(8,128)} custom-call(f32[8,128,128]{2,1,0:T(8,128)} %get-tuple-element.10.refs_0_, s16[8,128,128]{2,1,0:T(8,128)(2,1)} %get-tuple-element.11.refs_1_, f32[2,8,128,128]{3,2,1,0:T(8,128)} %get-tuple-element.12.refs_2_, s16[8,256,128]{2,1,0:T(8,128)(2,1)} %get-tuple-element.13.refs_3_, ...), custom_call_target="tpu_custom_call" | custom-call | tf_op jit(solution)/shard_map/pallas_call | solution.py:673
